TPU v7x, 1024 devices: a whole 8x8x8 slice. The times are simulated.
1024 devices in a mesh: seq: 128 (over y_hi, z, x), mp: 4 (over y_lo), role: 2 (over core).
Axes of the slice: x: 8, y: 8 (y_hi: 2, y_lo: 4; y = y_hi * 4 + y_lo), z: 8, core: 2. Of those that a mesh axis runs over, the one named last changes fastest.
Arguments:
- gen_hidden: bfloat16 [128, 256, 3072], P('seq', None, ('mp', 'role')), may hold values from -6 to 6
- gen_out_weight: bfloat16 [3072, 128], P(('mp', 'role')), may hold values from -0.109375 to 0.109375
- patch_order: int32 [128], replicated, may hold values from 0 to 127, each once
- frame_block: int32 [256], replicated, may hold values from 0 to 128, as said below
- embed_weight: bfloat16 [128, 3072], replicated, may hold values from -0.5 to 0.5
- pos_table: bfloat16 [128, 3072], replicated, may hold values from -3 to 3
- norm_gain: bfloat16 [3072], replicated, may hold values from 0.099609375 to 1.8984375
- qkv_weight: bfloat16 [3072, 3, 2048], P(None, None, ('mp', 'role')), may hold values from -0.109375 to 0.109375
- out_weight: bfloat16 [2048, 3072], P(('mp', 'role')), may hold values from -0.125 to 0.125
Outputs:
- disc_out: bfloat16 [32768, 3072], P(('seq', 'mp', 'role'))
Inputs may be any that keep to these rules, and one draw needn't show every extreme that they name: `patch_order`: each patch position appears in exactly one slot. `frame_block`: blocks are runs of consecutive frames with indices never falling, each of 1 to 4 frames, at least one of exactly 4; frames share a block iff their indices are equal.
All inputs are finite; a program needn't handle non-finite values.
Results may differ from a plain program's by a relative error of at most 0.006.
Values may be sent and summed in bfloat16 or wider, within the bound.
A program may use at most 64 MiB of HBM per device.

v0:
```python
import jax
import jax.numpy as jnp
from jax import lax
from jax.sharding import PartitionSpec as P

HS = 128
MOSTB = 4


def cut_along(array, dim, size):
    lengths = array.shape
    pieces = array.reshape(*lengths[:dim], size, lengths[dim] // size, *lengths[dim + 1 :])
    return jnp.moveaxis(pieces, dim, 0)


def sent_and_summed(array, axis, dim):
    pieces = cut_along(array, dim, lax.axis_size(axis))
    arrived = lax.all_to_all(pieces, axis, split_axis=0, concat_axis=0, tiled=True)
    return arrived.sum(axis=0)


def in_order(pieces, dim):
    pieces = jnp.moveaxis(pieces, 0, dim)
    lengths = pieces.shape
    return pieces.reshape(*lengths[:dim], lengths[dim] * lengths[dim + 1], *lengths[dim + 2 :])


def copy_for_each(array, axis):
    size = lax.axis_size(axis)
    return lax.all_to_all(
        jnp.broadcast_to(array[None], (size, *array.shape)), axis, 0, 0, tiled=True
    )


def gather_directly(array, axis, dim):
    return in_order(copy_for_each(array, axis), dim)


def from_behind(block, axis, distance):
    devices = range(lax.axis_size(axis))
    route = [(i - distance, i) for i in devices if i - distance in devices]
    return lax.ppermute(block, axis, route)


def prepare(latents, embed_weight, pos_table, norm_gain, qkv_weight):
    frames, patches, channels = latents.shape
    flat = latents.reshape(frames * patches, channels)
    embedded = jnp.dot(flat, embed_weight, preferred_element_type=jnp.float32).reshape(
        frames, patches, -1
    )
    embedded = embedded + pos_table.astype(jnp.float32)[None]
    scale = lax.rsqrt(jnp.mean(embedded * embedded, axis=-1, keepdims=True) + 1e-06)
    normed = (embedded * scale * norm_gain.astype(jnp.float32)).astype(jnp.bfloat16)
    proj = jnp.einsum("fpd,dcm->cfpm", normed, qkv_weight, preferred_element_type=jnp.float32)
    return (embedded, proj.astype(jnp.bfloat16))


def lookup_blocks(frame_ids, frame_block):
    table = jnp.arange(frame_block.shape[0], dtype=jnp.int32)
    hit = frame_ids[:, None] == table[None, :]
    found = jnp.sum(jnp.where(hit, frame_block[None, :], 0), axis=1)
    return jnp.where(jnp.any(hit, axis=1), found, -1)


def on_device(
    gen_hidden,
    gen_out_weight,
    patch_order,
    frame_block,
    embed_weight,
    pos_table,
    norm_gain,
    qkv_weight,
    out_weight,
):
    partial_latents = jnp.einsum(
        "sfd,dc->sfc", gen_hidden, gen_out_weight, preferred_element_type=jnp.float32
    )
    share = sent_and_summed(partial_latents, ("mp", "role"), 2).astype(jnp.bfloat16)
    moved_share = lax.all_to_all(share, "seq", split_axis=1, concat_axis=0, tiled=True)
    moved = gather_directly(moved_share, ("mp", "role"), 2)
    patches = moved.shape[0]
    frame_dev = moved.shape[1]
    inverse = (
        jnp.zeros((patches,), jnp.int32).at[patch_order].set(jnp.arange(patches, dtype=jnp.int32))
    )
    own_latents = jnp.transpose(moved[inverse], (1, 0, 2))
    reach = (MOSTB - 2) // frame_dev + 1
    head_cols = qkv_weight.shape[2]
    embedded, proj = prepare(own_latents, embed_weight, pos_table, norm_gain, qkv_weight)
    query = proj[0]
    own_kv = proj[1:]
    pieces = []
    for offset in range(-reach, reach + 1):
        if offset == 0:
            pieces.append(own_kv)
        else:
            pieces.append(from_behind(own_kv, "seq", -offset))
    window_kv = jnp.concatenate(pieces, axis=1)
    heads_here = head_cols // HS
    rows = frame_dev * patches
    key_frames = window_kv.shape[1]
    device = lax.axis_index("seq")
    query_ids = device * frame_dev + jnp.arange(frame_dev, dtype=jnp.int32)
    key_ids = (device - reach) * frame_dev + jnp.arange(key_frames, dtype=jnp.int32)
    query_blocks = lookup_blocks(query_ids, frame_block)
    key_blocks = lookup_blocks(key_ids, frame_block)
    frame_mask = query_blocks[:, None] == key_blocks[None, :]
    mask = jnp.repeat(jnp.repeat(frame_mask, patches, axis=0), patches, axis=1)
    query_rows = query.reshape(rows, heads_here, HS)
    key_rows = window_kv[0].reshape(key_frames * patches, heads_here, HS)
    value_rows = window_kv[1].reshape(key_frames * patches, heads_here, HS)
    scores = jnp.einsum(
        "qhe,khe->hqk", query_rows, key_rows, preferred_element_type=jnp.float32
    ) / jnp.sqrt(jnp.float32(HS))
    scores = jnp.where(mask[None], scores, jnp.float32(-1e30))
    top = jnp.max(scores, axis=-1, keepdims=True)
    expo = jnp.where(mask[None], jnp.exp(scores - top), jnp.float32(0.0))
    probs = (expo / jnp.sum(expo, axis=-1, keepdims=True)).astype(jnp.bfloat16)
    attn = jnp.einsum("hqk,khe->qhe", probs, value_rows, preferred_element_type=jnp.float32)
    attn = attn.astype(jnp.bfloat16).reshape(rows, head_cols)
    group = lax.axis_size(("mp", "role"))
    share_rows = rows // group
    core_count = lax.axis_size("role")
    chip_count = lax.axis_size("mp")
    arranged = jnp.transpose(
        attn.reshape(chip_count, core_count, share_rows, head_cols), (1, 0, 2, 3)
    ).reshape(rows, head_cols)
    halves = sent_and_summed(
        jnp.dot(arranged, out_weight, preferred_element_type=jnp.float32), "role", 0
    )
    mixed = sent_and_summed(halves, "mp", 0)
    flat_embedded = embedded.reshape(rows, -1)
    mine = lax.dynamic_slice_in_dim(
        flat_embedded, lax.axis_index(("mp", "role")) * share_rows, share_rows, 0
    )
    return (mine + mixed).astype(jnp.bfloat16)


def solution(mesh):
    in_specs = (
        P("seq", None, ("mp", "role")),
        P(("mp", "role"), None),
        P(),
        P(),
        P(),
        P(),
        P(),
        P(None, None, ("mp", "role")),
        P(("mp", "role"), None),
    )
    out_specs = P(("seq", "mp", "role"), None)
    return jax.shard_map(
        on_device, mesh=mesh, in_specs=in_specs, out_specs=out_specs, check_vma=False
    )
```

profile of v0, /device:TPU:112, one launch (start us, length us, event | category | flops | bytes accessed | tf_op | source)
XLA Modules:
  0.0 170.1 jit_solution(5725583231668773952)
XLA Ops:
  0.0 1.1 copy.47
  1.1 1.8 %convolution_bitcast_fusion = f32[8,1,256,16]{2,3,1,0:T(8,128)} fusion(bf16[8,16,384]{2,1,0:T(8,128)(2,1)S(1)} %bitcast.82, bf16[1,256,384]{2,1,0:T(8,128)(2,1)} %param.9), kind=kOutput, calls=%fused_computation.23 | convolution fusion | flops 25165824 | bytes 425984 | tf_op jit(solution)/shard_map/sfd,dc->sfc/dot_general | solution.py:76
  2.9 5.9 %all-to-all-start = ((f32[8,1,256,16]{2,3,1,0:T(8,128)}), f32[8,1,256,16]{2,3,1,0:T(8,128)S(1)}, u32[]{:S(2)}, u32[]{:S(2)}) async-start(f32[8,1,256,16]{2,3,1,0:T(8,128)} %convolution_bitcast_fusion), calls=%async_computation | async-start | bytes 262144 | tf_op jit(solution)/shard_map/all_to_all | solution.py:18
  9.0 0.9 select_reduce_fusion
  9.9 0.9 select_reduce_fusion.1
  10.9 2.2 %all-to-all-done = f32[8,1,256,16]{2,3,1,0:T(8,128)S(1)} async-done(((f32[8,1,256,16]{2,3,1,0:T(8,128)}), f32[8,1,256,16]{2,3,1,0:T(8,128)S(1)}, u32[]{:S(2)}, u32[]{:S(2)}) %all-to-all-start) | async-done | bytes 131104 | tf_op jit(solution)/shard_map/all_to_all | solution.py:18
  13.2 0.8 copy.50
  14.0 28.6 %all-to-all-start.1 = ((bf16[1,256,16]{2,0,1:T(2,128)(2,1)}), bf16[1,256,16]{2,0,1:T(2,128)(2,1)S(1)}, u32[]{:S(2)}, u32[]{:S(2)}) async-start(bf16[1,256,16]{2,0,1:T(2,128)(2,1)} %copy.50), calls=%async_computation.1 | async-start | bytes 262144 | tf_op jit(solution)/shard_map/all_to_all | solution.py:80
  43.3 1.0 scatter_custom_fusion
  44.2 10.9 %all-to-all-done.1 = bf16[1,256,16]{2,0,1:T(2,128)(2,1)S(1)} async-done(((bf16[1,256,16]{2,0,1:T(2,128)(2,1)}), bf16[1,256,16]{2,0,1:T(2,128)(2,1)S(1)}, u32[]{:S(2)}, u32[]{:S(2)}) %all-to-all-start.1) | async-done | bytes 8224 | tf_op jit(solution)/shard_map/all_to_all | solution.py:80
  55.9 5.7 %all-to-all-start.2 = ((bf16[8,128,2,16]{1,3,2,0:T(8,128)(2,1)}), bf16[8,128,2,16]{1,3,2,0:T(8,128)(2,1)S(1)}, u32[]{:S(2)}, u32[]{:S(2)}) async-start(bf16[8,128,2,16]{1,3,2,0:T(8,128)(2,1)} %broadcast_in_dim.86), calls=%async_computation.2 | async-start | bytes 131072 | tf_op jit(solution)/shard_map/all_to_all | solution.py:30
  62.3 1.3 convert_element_type.43
  63.6 0.9 all-to-all-done.2
  64.7 0.7 gather_fusion
  65.4 1.9 %multiply_reduce_fusion = (f32[2,128]{1,0:T(2,128)S(1)}, f32[2,128,3072]{2,1,0:T(8,128)S(1)}) fusion(f32[128,3072]{1,0:T(8,128)S(1)} %convert_element_type.43, bf16[128,3072]{1,0:T(8,128)(2,1)} %param.13, bf16[2,128,128]{2,0,1:T(2,128)(2,1)S(1)} %bitcast.83), kind=kOutput, calls=%fused_computation.12 | convolution fusion | flops 203685632 | bytes 5571584 | tf_op jit(solution)/shard_map/dot_general | solution.py:48
  68.0 1.5 fusion.19
  69.5 2.2 %collective-permute-start = (bf16[2,2,128,256]{3,2,0,1:T(8,128)(2,1)S(1)}, bf16[2,2,128,256]{3,2,0,1:T(8,128)(2,1)S(1)}, u32[]{:S(2)}, u32[]{:S(2)}) collective-permute-start(bf16[2,2,128,256]{3,2,0,1:T(8,128)(2,1)S(1)} %slice.18), channel_id=1, source_target_pairs={{0,16},{8,24},{16,32},{24,40},{32,48},{40,56},{48,64},{56,72},{64,... | collective-permute-start | bytes 786440 | tf_op jit(solution)/shard_map/ppermute | solution.py:42
  71.8 2.6 %collective-permute-start.1 = (bf16[2,2,128,256]{3,2,0,1:T(8,128)(2,1)S(1)}, bf16[2,2,128,256]{3,2,0,1:T(8,128)(2,1)S(1)}, u32[]{:S(2)}, u32[]{:S(2)}) collective-permute-start(bf16[2,2,128,256]{3,2,0,1:T(8,128)(2,1)S(1)} %slice.18), channel_id=1, source_target_pairs={{0,8},{8,16},{16,24},{24,32},{32,40},{40,48},{48,56},{56,64},{64,7... | collective-permute-start | bytes 786440 | tf_op jit(solution)/shard_map/ppermute | solution.py:42
  74.6 1.1 copy.55
  75.7 12.7 %collective-permute-start.3 = (bf16[2,2,128,256]{3,2,0,1:T(8,128)(2,1)S(1)}, bf16[2,2,128,256]{3,2,0,1:T(8,128)(2,1)S(1)}, u32[]{:S(2)}, u32[]{:S(2)}) collective-permute-start(bf16[2,2,128,256]{3,2,0,1:T(8,128)(2,1)S(1)} %slice.18), channel_id=1, source_target_pairs={{16,0},{24,8},{32,16},{40,24},{48,32},{56,40},{64,48},{72,56},{80,... | collective-permute-start | bytes 786440 | tf_op jit(solution)/shard_map/ppermute | solution.py:42
  88.4 3.3 %collective-permute-start.2 = (bf16[2,2,128,256]{3,2,0,1:T(8,128)(2,1)S(1)}, bf16[2,2,128,256]{3,2,0,1:T(8,128)(2,1)}, u32[]{:S(2)}, u32[]{:S(2)}) collective-permute-start(bf16[2,2,128,256]{3,2,0,1:T(8,128)(2,1)S(1)} %slice.18), channel_id=1, source_target_pairs={{8,0},{16,8},{24,16},{32,24},{40,32},{48,40},{56,48},{64,56},{72,6... | collective-permute-start | bytes 786440 | tf_op jit(solution)/shard_map/ppermute | solution.py:42
  92.4 4.4 %collective-permute-done = bf16[2,2,128,256]{3,2,0,1:T(8,128)(2,1)S(1)} collective-permute-done((bf16[2,2,128,256]{3,2,0,1:T(8,128)(2,1)S(1)}, bf16[2,2,128,256]{3,2,0,1:T(8,128)(2,1)S(1)}, u32[]{:S(2)}, u32[]{:S(2)}) %collective-permute-start) | collective-permute-done | bytes 262176 | tf_op jit(solution)/shard_map/ppermute | solution.py:42
  96.8 9.1 %collective-permute-done.1 = bf16[2,2,128,256]{3,2,0,1:T(8,128)(2,1)S(1)} collective-permute-done((bf16[2,2,128,256]{3,2,0,1:T(8,128)(2,1)S(1)}, bf16[2,2,128,256]{3,2,0,1:T(8,128)(2,1)S(1)}, u32[]{:S(2)}, u32[]{:S(2)}) %collective-permute-start.1) | collective-permute-done | bytes 262176 | tf_op jit(solution)/shard_map/ppermute | solution.py:42
  105.9 1.1 collective-permute-done.2
  107.0 1.0 constant_dynamic-update-slice_fusion.1
  108.4 4.0 %fusion.48 = (f32[2,256]{1,0:T(2,128)S(1)}, f32[2,256,1280]{2,1,0:T(8,128)}) fusion(pred[256,1280]{1,0:T(8,128)(4,1)} %copy.55, bf16[1280,2,128]{2,1,0:T(2,128)(2,1)S(1)} %reshape_squeeze.11, bf16[256,2,128]{2,1,0:T(2,128)(2,1)} %reshape_squeeze.10), kind=kOutput, calls=%fused_computation.62 | convolution fusion | flops 171050240 | bytes 3737600 | tf_op jit(solution)/shard_map/sub | solution.py:118
  112.4 2.4 %fusion.25 = bf16[256,2,128]{0,2,1:T(8,128)(2,1)S(1)} fusion(f32[2,256,1280]{2,1,0:T(8,128)} %get-tuple-element.10, f32[2,256]{1,0:T(2,128)S(1)} %get-tuple-element.9, bf16[1280,2,128]{2,1,0:T(2,128)(2,1)S(1)} %reshape_squeeze.9), kind=kOutput, calls=%fused_computation.24 | convolution fusion | flops 169148416 | bytes 3409920 | tf_op jit(solution)/shard_map/hqk,khe->qhe/dot_general | solution.py:120
  115.6 7.2 %all_to_all.29 = f32[2,128,3072]{2,1,0:T(8,128)} all-to-all(f32[2,128,3072]{2,1,0:T(8,128)S(1)} %fusion.9), channel_id=1, replica_groups=mesh['seq'=128,'mp'=4,'role'=2] {'role'}, dimensions={0} | all-to-all | bytes 6291456 | tf_op jit(solution)/shard_map/all_to_all | solution.py:18
  122.9 3.4 %reduce_sum.68 = f32[128,3072]{1,0:T(8,128)} reduce(f32[2,128,3072]{2,1,0:T(8,128)} %all_to_all.29, f32[]{:T(128)} %constant.17.clone.1), dimensions={0}, to_apply=%region_9.10 | reduce | flops 393216 | bytes 4718596 | tf_op jit(solution)/shard_map/reduce_sum | solution.py:19
  126.3 6.3 %all-to-all-start.4 = ((f32[4,32,3072]{2,1,0:T(8,128)}), f32[4,32,3072]{2,1,0:T(8,128)S(1)}, u32[]{:S(2)}, u32[]{:S(2)}) async-start(f32[4,32,3072]{2,1,0:T(8,128)} %bitcast.77), calls=%async_computation.4 | async-start | bytes 3145728 | tf_op jit(solution)/shard_map/all_to_all | solution.py:18
  132.5 35.7 %all-to-all-done.4 = f32[4,32,3072]{2,1,0:T(8,128)S(1)} async-done(((f32[4,32,3072]{2,1,0:T(8,128)}), f32[4,32,3072]{2,1,0:T(8,128)S(1)}, u32[]{:S(2)}, u32[]{:S(2)}) %all-to-all-start.4) | async-done | bytes 1572896 | tf_op jit(solution)/shard_map/all_to_all | solution.py:18
  168.4 1.7 %add_convert_fusion = bf16[32,3072]{1,0:T(8,128)(2,1)} fusion(f32[32,3072]{1,0:T(8,128)S(1)} %reduce_sum.69, f32[256,3072]{1,0:T(8,128)} %bitcast.78, s32[]{:T(128)S(6)} %select_n.42), kind=kLoop, calls=%fused_computation.28 | loop fusion | flops 196608 | bytes 983044 | tf_op jit(solution)/shard_map/convert_element_type | solution.py:137
  (45 shorter events, 5.6 us)
Async XLA Ops:
  0.0 115.1 %copy-start = (bf16[256,3072]{1,0:T(8,128)(2,1)S(1)}, bf16[256,3072]{1,0:T(8,128)(2,1)}, u32[]{:S(2)}) copy-start(bf16[256,3072]{1,0:T(8,128)(2,1)} %param.17) | copy-start | bytes 4718596
  2.9 10.2 %all-to-all-start = ((f32[8,1,256,16]{2,3,1,0:T(8,128)}), f32[8,1,256,16]{2,3,1,0:T(8,128)S(1)}, u32[]{:S(2)}, u32[]{:S(2)}) async-start(f32[8,1,256,16]{2,3,1,0:T(8,128)} %convolution_bitcast_fusion), calls=%async_computation | async-start | bytes 262144 | tf_op jit(solution)/shard_map/all_to_all | solution.py:18
  14.0 41.2 %all-to-all-start.1 = ((bf16[1,256,16]{2,0,1:T(2,128)(2,1)}), bf16[1,256,16]{2,0,1:T(2,128)(2,1)S(1)}, u32[]{:S(2)}, u32[]{:S(2)}) async-start(bf16[1,256,16]{2,0,1:T(2,128)(2,1)} %copy.50), calls=%async_computation.1 | async-start | bytes 262144 | tf_op jit(solution)/shard_map/all_to_all | solution.py:80
  55.9 8.6 %all-to-all-start.2 = ((bf16[8,128,2,16]{1,3,2,0:T(8,128)(2,1)}), bf16[8,128,2,16]{1,3,2,0:T(8,128)(2,1)S(1)}, u32[]{:S(2)}, u32[]{:S(2)}) async-start(bf16[8,128,2,16]{1,3,2,0:T(8,128)(2,1)} %broadcast_in_dim.86), calls=%async_computation.2 | async-start | bytes 131072 | tf_op jit(solution)/shard_map/all_to_all | solution.py:30
  65.4 2.6 %copy-start.2 = (bf16[3072,3,256]{2,0,1:T(8,128)(2,1)S(1)}, bf16[3072,3,256]{2,0,1:T(8,128)(2,1)}, u32[]{:S(2)}) copy-start(bf16[3072,3,256]{2,0,1:T(8,128)(2,1)} %param.16) | copy-start | bytes 14155780
  67.4 2.1 %copy-start.1 = (f32[2,128,3072]{2,1,0:T(8,128)}, f32[2,128,3072]{2,1,0:T(8,128)S(1)}, u32[]{:S(2)}) copy-start(f32[2,128,3072]{2,1,0:T(8,128)S(1)} %get-tuple-element.8) | copy-start | bytes 9437188
  69.5 27.2 %collective-permute-start = (bf16[2,2,128,256]{3,2,0,1:T(8,128)(2,1)S(1)}, bf16[2,2,128,256]{3,2,0,1:T(8,128)(2,1)S(1)}, u32[]{:S(2)}, u32[]{:S(2)}) collective-permute-start(bf16[2,2,128,256]{3,2,0,1:T(8,128)(2,1)S(1)} %slice.18), channel_id=1, source_target_pairs={{0,16},{8,24},{16,32},{24,40},{32,48},{40,56},{48,64},{56,72},{64,... | collective-permute-start | bytes 786440 | tf_op jit(solution)/shard_map/ppermute | solution.py:42
  71.8 34.1 %collective-permute-start.1 = (bf16[2,2,128,256]{3,2,0,1:T(8,128)(2,1)S(1)}, bf16[2,2,128,256]{3,2,0,1:T(8,128)(2,1)S(1)}, u32[]{:S(2)}, u32[]{:S(2)}) collective-permute-start(bf16[2,2,128,256]{3,2,0,1:T(8,128)(2,1)S(1)} %slice.18), channel_id=1, source_target_pairs={{0,8},{8,16},{16,24},{24,32},{32,40},{40,48},{48,56},{56,64},{64,7... | collective-permute-start | bytes 786440 | tf_op jit(solution)/shard_map/ppermute | solution.py:42
  75.7 32.2 %collective-permute-start.3 = (bf16[2,2,128,256]{3,2,0,1:T(8,128)(2,1)S(1)}, bf16[2,2,128,256]{3,2,0,1:T(8,128)(2,1)S(1)}, u32[]{:S(2)}, u32[]{:S(2)}) collective-permute-start(bf16[2,2,128,256]{3,2,0,1:T(8,128)(2,1)S(1)} %slice.18), channel_id=1, source_target_pairs={{16,0},{24,8},{32,16},{40,24},{48,32},{56,40},{64,48},{72,56},{80,... | collective-permute-start | bytes 786440 | tf_op jit(solution)/shard_map/ppermute | solution.py:42
  88.4 18.6 %collective-permute-start.2 = (bf16[2,2,128,256]{3,2,0,1:T(8,128)(2,1)S(1)}, bf16[2,2,128,256]{3,2,0,1:T(8,128)(2,1)}, u32[]{:S(2)}, u32[]{:S(2)}) collective-permute-start(bf16[2,2,128,256]{3,2,0,1:T(8,128)(2,1)S(1)} %slice.18), channel_id=1, source_target_pairs={{8,0},{16,8},{24,16},{32,24},{40,32},{48,40},{56,48},{64,56},{72,6... | collective-permute-start | bytes 786440 | tf_op jit(solution)/shard_map/ppermute | solution.py:42
  126.3 42.0 %all-to-all-start.4 = ((f32[4,32,3072]{2,1,0:T(8,128)}), f32[4,32,3072]{2,1,0:T(8,128)S(1)}, u32[]{:S(2)}, u32[]{:S(2)}) async-start(f32[4,32,3072]{2,1,0:T(8,128)} %bitcast.77), calls=%async_computation.4 | async-start | bytes 3145728 | tf_op jit(solution)/shard_map/all_to_all | solution.py:18
where the time goes:
time: 171 us; the launch traced here: 170 us
  starting transfers between devices  67.2 us (39%)
  waiting for transfers between devices  64.3 us (38%)
  matrix products  12.2 us (7%)
  other arithmetic  10.1 us (6%)
  local copies, waits for them, and re-layouts  8.81 us (5%)
  blocking collectives  7.21 us (4%)
    all_to_all x2, waiting for transfers between devices, sent_and_summed(): lax.all_to_all(pieces, axis, split_axis=0, concat_axis=0, tiled=True)  37.9 us
    all_to_all x1, starting transfers between devices, on_device(): lax.all_to_all(share, 'seq', split_axis=1, concat_axis=0, tiled=True)  28.6 us
    ppermute x4, starting transfers between devices, from_behind(): return lax.ppermute(block, axis, route)  20.7 us
    ppermute x4, waiting for transfers between devices, from_behind(): return lax.ppermute(block, axis, route)  14.5 us
    all_to_all x2, starting transfers between devices, sent_and_summed(): lax.all_to_all(pieces, axis, split_axis=0, concat_axis=0, tiled=True)  12.2 us
    all_to_all x1, waiting for transfers between devices, on_device(): lax.all_to_all(share, 'seq', split_axis=1, concat_axis=0, tiled=True)  10.9 us
    all_to_all x1, blocking collectives, sent_and_summed(): lax.all_to_all(pieces, axis, split_axis=0, concat_axis=0, tiled=True)  7.21 us
    all_to_all x1, starting transfers between devices, copy_for_each(): lax.all_to_all(jnp.broadcast_to(array[None], (size, *array.shape)), axis,...  5.7 us
  transfers between devices with their start and end apart: 8, of which 7 were waited for; matrix products, arithmetic and copies ran while one was open for 5% of the time, Pallas kernels for 0%

commit v1 on v0

v1 whole, which is shorter than its diff:
```python
import functools

import jax
import jax.numpy as jnp
from jax import lax
from jax.experimental import pallas as pl
from jax.experimental.pallas import tpu as pltpu
from jax.sharding import PartitionSpec as P

MESH = pl.DeviceIdType.MESH
F32 = jnp.float32
BF16 = jnp.bfloat16
HS = 128
CHUNKS = 4
NEG = -1e30


def dot(a, b, precision=None):
    return jnp.dot(a, b, preferred_element_type=F32, precision=precision)


def dot_t(a, b, precision=None):
    return lax.dot_general(
        a, b, (((1,), (1,)), ((), ())), preferred_element_type=F32, precision=precision
    )


def split2(a):
    hi = a.astype(BF16)
    return hi, (a - hi.astype(F32)).astype(BF16)


def iota(shape, dim):
    return lax.broadcasted_iota(jnp.int32, shape, dim)


def kernel(
    gh_hbm,
    gw_hbm,
    po_ref,
    fb_ref,
    e_hbm,
    pos_hbm,
    gain_ref,
    w_hbm,
    wo_hbm,
    out_ref,
    gh,
    gw,
    e,
    pos,
    w,
    wo,
    ppad,
    send_a,
    recv_a,
    send_x,
    recv_x,
    send_z,
    lat,
    kv,
    fhl,
    m_all,
    fv_all,
    sel_q,
    hr2,
    he2,
    ncol,
    nlane,
    bias,
    gg,
    lat_q,
    q_all,
    u_all,
    a_all,
    acc,
    send_c,
    recv_c,
    load_sem,
    sa,
    ra,
    sx,
    rx,
    sz,
    rz,
    sf,
    rf,
    sp,
    rp,
    sc,
    rc,
):
    seq = lax.axis_index("seq")
    m = lax.axis_index("mp")
    r = lax.axis_index("role")
    ys = seq // 64
    z = (seq // 8) % 8
    x = seq % 8
    j = 2 * m + r
    y = ys * 4 + m
    is_self = jnp.logical_and(j == z, True)

    def group(k):
        return (seq, k // 2, k % 2)

    def row_x(x2):
        return (ys * 64 + z * 8 + x2, m, r)

    def ring(y2, role):
        return ((y2 // 4) * 64 + z * 8 + x, y2 % 4, role)

    def zy_source(idx):
        return ((idx // 4) * 64 + (2 * (idx % 4) + r) * 8 + x, z // 2, z % 2)

    def zy_dest(i):
        y2 = (y + i) % 8
        return ((y2 // 4) * 64 + j * 8 + x, y2 % 4, z % 2)

    partner = (seq, m, 1 - r)

    barrier = pltpu.get_barrier_semaphore()

    def greet(device):
        pl.semaphore_signal(barrier, inc=1, device_id=device, device_id_type=MESH)

    for step in range(1, 8):
        greet(group((j + step) % 8))
        greet(row_x((x + step) % 8))
    for idx in range(8):
        here = jnp.logical_and(is_self, idx == ys * 4 + z // 2)

        @pl.when(jnp.logical_not(here))
        def _():
            greet(zy_source(idx))

    for step in range(1, 4):
        i = (1 + r + step) % 4
        greet(ring((y + 1 + r - i + 8) % 8, r))

    def load(src, dst, n):
        return pltpu.make_async_copy(src, dst, load_sem.at[n])

    loads = [
        load(gh_hbm, gh, 0),
        load(gw_hbm, gw, 1),
        load(e_hbm, e, 2),
        load(pos_hbm, pos, 3),
        load(w_hbm, w, 4),
        load(wo_hbm, wo.at[r], 5),
    ]
    for copy in loads:
        copy.start()

    ppad[0:8, :] = jnp.zeros((8, 128), F32)
    ppad[264:288, :] = jnp.zeros((24, 128), F32)

    po_f = jnp.broadcast_to(po_ref[...], (16, 128)).astype(F32).astype(BF16)
    spread = (iota((128, 1024), 0) == lax.shift_right_logical(iota((128, 1024), 1), 3)).astype(
        F32
    ).astype(BF16)
    po_lane = dot(po_f, spread)[0:1]
    perm_t = (jnp.broadcast_to(po_ref[...], (128, 128)) == iota((128, 128), 0)).astype(F32).astype(
        BF16
    )
    rows8 = (lax.shift_right_logical(iota((1024, 128), 0), 3) == iota((1024, 128), 1)).astype(
        F32
    ).astype(BF16)
    onehot = dot_t(rows8, perm_t).astype(BF16)
    kv[0, :, 128:256] = onehot
    kv[1, :, 128:256] = onehot
    w_lane = jnp.bitwise_and(iota((1, 1024), 1), 7)
    for yt in range(2):
        base = yt * 128 + z * 16 + x * 2 - 3
        blocks = []
        key_block = jnp.full((1, 1024), -1, jnp.int32)
        for n in range(8):
            frame = base + n
            value = fb_ref[jnp.clip(frame, 0, 255)]
            value = jnp.where(jnp.logical_and(frame >= 0, frame <= 255), value, -1)
            blocks.append(value)
            key_block = jnp.where(w_lane == n, value, key_block)
        for fi in range(2):
            bias[yt, fi] = jnp.where(key_block == blocks[3 + fi], F32(0), F32(NEG))
    for i in range(4):
        d = (y - 1 - r + i + 8) % 8
        fi = (d % 4) // 2
        patch = ((d % 2) * 2 + r) * 32
        rows = (iota((32, 1024), 0) + patch).astype(F32)
        hit = jnp.logical_and(
            jnp.broadcast_to(po_lane, (32, 1024)) == rows,
            jnp.broadcast_to(w_lane, (32, 1024)) == 3 + fi,
        )
        sel_q[i] = hit.astype(F32).astype(BF16)

    loads[0].wait()
    loads[1].wait()
    ppad[8:264, :] = dot(gh[...], gw[...])
    for k in range(8):
        for yt in range(2):
            first = 128 * yt + 16 * k + 5
            send_a[k, 24 * yt : 24 * yt + 24, :] = ppad[first : first + 24, :]

    pl.semaphore_wait(barrier, 25 - is_self.astype(jnp.int32))

    def copy_a(step):
        k = (j + step) % 8
        return pltpu.make_async_remote_copy(
            send_a.at[k], recv_a.at[j], sa.at[step], ra.at[j], group(k), MESH
        )

    def land_a(step):
        k = (j + step) % 8
        return pltpu.make_async_remote_copy(
            send_a.at[k], recv_a.at[k], sa.at[step], ra.at[k], group(k), MESH
        )

    for step in range(1, 8):
        copy_a(step).start()
    loads[5].wait()
    wo_copy = pltpu.make_async_remote_copy(
        wo.at[r], wo.at[r], sp.at[0], rp.at[0], partner, MESH
    )
    wo_copy.start()

    loads[2].wait()
    loads[3].wait()
    gain = gain_ref[...].astype(F32)
    for n, table in enumerate((e, pos)):
        hi, lo = split2(table[...].astype(F32) * gain)
        fhl[n * 128 : n * 128 + 128, :] = hi
        fhl[256 + n * 128 : 384 + n * 128, :] = lo
    ghi, glo = split2(dot_t(e[...], e[...]))
    gg[:, 0:128] = ghi
    gg[:, 128:256] = glo
    he = 2.0 * dot_t(pos[...], e[...])
    he2[...] = he
    he_hi, he_lo = split2(he)
    hr2[...] = dot(onehot, he_hi) + dot(onehot, he_lo)
    norms = dot_t(pos[...], pos[...])
    diagonal = jnp.where(iota((128, 128), 0) == iota((128, 128), 1), norms, F32(0))
    ncol[...] = jnp.broadcast_to(jnp.sum(diagonal, axis=1, keepdims=True), (128, 128))
    nrow = jnp.broadcast_to(jnp.sum(diagonal, axis=0, keepdims=True), (8, 128))
    nlane[...] = dot_t(nrow, onehot.astype(F32), lax.Precision.HIGHEST)[0:1]
    loads[4].wait()

    def weight_product(c):
        both = dot(fhl[...], w[c])
        return both[0:256] + both[256:512]

    for step in range(1, 8):
        land_a(step).wait_recv()
    total = send_a[j]
    for step in range(1, 8):
        total = total + recv_a[(j + step) % 8]
    recv_a[j] = total
    for n in range(8):
        halves = [recv_a[j, 24 * yt + 2 * n : 24 * yt + 2 * n + 8, :] for yt in range(2)]
        send_x[n] = jnp.concatenate(halves, axis=0).astype(BF16)

    def copy_x(step):
        x2 = (x + step) % 8
        return pltpu.make_async_remote_copy(
            send_x.at[x2], recv_x.at[x], sx.at[step], rx.at[x], row_x(x2), MESH
        )

    def land_x(step):
        x2 = (x + step) % 8
        return pltpu.make_async_remote_copy(
            send_x.at[x2], recv_x.at[x2], sx.at[step], rx.at[x2], row_x(x2), MESH
        )

    for step in range(1, 8):
        copy_x(step).start()
    recv_x[x] = send_x[x]

    fq = weight_product(0)
    fk = weight_product(1)

    for step in range(1, 8):
        land_x(step).wait_recv()
    for a in range(4):
        first = recv_x[2 * a].astype(F32)
        second = recv_x[2 * a + 1].astype(F32)
        for yt in range(2):
            pair = jnp.concatenate(
                [first[8 * yt : 8 * yt + 8], second[8 * yt : 8 * yt + 8]], axis=0
            )
            send_z[yt, 16 * a : 16 * a + 16, :] = pair.astype(BF16)

    own_block = ys * 8 + z
    own_idx = ys * 4 + z // 2

    def copy_z(i):
        return pltpu.make_async_remote_copy(
            send_z, lat.at[:, own_block], sz.at[i], rz.at[own_idx], zy_dest(i), MESH
        )

    local_z = pltpu.make_async_copy(send_z, lat.at[:, own_block], rz.at[own_idx])
    for i in range(1, 8):
        copy_z(i).start()

    @pl.when(jnp.logical_not(is_self))
    def _():
        copy_z(0).start()

    @pl.when(is_self)
    def _():
        local_z.start()

    for h in range(2):
        cols = slice(HS * h, HS * h + HS)
        bil = dot_t(fq[:, cols], fk[:, cols], lax.Precision.HIGHEST)
        hi, lo = split2(bil)
        m_all[r, 0, :, 256 * h : 256 * h + 256] = hi
        m_all[r, 1, :, 256 * h : 256 * h + 256] = lo
    hi, lo = split2(weight_product(2))
    fv_all[r, 0] = hi
    fv_all[r, 1] = lo
    m_copy = pltpu.make_async_remote_copy(
        m_all.at[r], m_all.at[r], sp.at[1], rp.at[1], partner, MESH
    )
    f_copy = pltpu.make_async_remote_copy(
        fv_all.at[r], fv_all.at[r], sp.at[2], rp.at[2], partner, MESH
    )
    m_copy.start()
    f_copy.start()

    def block_of(idx, role):
        return (idx // 4) * 8 + 2 * (idx % 4) + role

    def forward(idx):
        b = block_of(idx, r)
        return pltpu.make_async_remote_copy(
            lat.at[:, b], lat.at[:, b], sf.at[idx], rf.at[idx], partner, MESH
        )

    def forwarded(idx):
        b = block_of(idx, 1 - r)
        return pltpu.make_async_remote_copy(
            lat.at[:, b], lat.at[:, b], sf.at[idx], rf.at[idx], partner, MESH
        )

    for idx in range(8):
        b = block_of(idx, r)
        pltpu.make_async_copy(lat.at[:, b], lat.at[:, b], rz.at[idx]).wait()
        forward(idx).start()
    for idx in range(8):
        forwarded(idx).wait_recv()

    scale_k = []
    ones = jnp.ones((8, 128), F32)
    for yt in range(2):
        rows = lat[yt].reshape(1024, 128)
        kv[yt, :, 0:128] = rows
        both = dot(rows, gg[...])
        z_part = rows.astype(F32) * (both[:, 0:128] + both[:, 128:256] + hr2[...])
        total = dot_t(ones, z_part, lax.Precision.HIGHEST)[0:1] + nlane[...]
        scale_k.append(lax.rsqrt(jnp.maximum(total, 0.0) * F32(1 / 3072) + F32(1e-06)))
    for yt in range(2):
        bias[yt, 2] = scale_k[yt]

    tokens = []
    scales = []
    for i in range(4):
        d = (y - 1 - r + i + 8) % 8
        patch = pl.multiple_of(((d % 2) * 2 + r) * 32, 32)
        mine = dot(sel_q[i], kv[d // 4, :, 0:128])
        lat_q[32 * i : 32 * i + 32, :] = mine.astype(BF16)
        both = dot(mine.astype(BF16), gg[...])
        squares = mine * (both[:, 0:128] + both[:, 128:256] + he2[pl.ds(patch, 32), :])
        total = jnp.sum(squares, axis=1, keepdims=True) + ncol[pl.ds(patch, 32), 0:1]
        scales.append(
            lax.rsqrt(jnp.maximum(total, 0.0) * F32(1 / 3072) + F32(1e-06))
            * F32(1 / HS**0.5)
        )
        place = (iota((32, 128), 0) + patch == iota((32, 128), 1)).astype(F32).astype(BF16)
        tokens.append(jnp.concatenate([mine.astype(BF16), place], axis=1))
    tokens = jnp.concatenate(tokens, axis=0)
    scales = jnp.concatenate(scales, axis=0)
    pltpu.make_async_remote_copy(
        m_all.at[1 - r], m_all.at[1 - r], sp.at[1], rp.at[1], partner, MESH
    ).wait_recv()
    for role in range(2):
        q = (dot(tokens, m_all[role, 0]) + dot(tokens, m_all[role, 1])) * scales
        for h in range(2):
            q_all[2 * role + h] = q[:, 256 * h : 256 * h + 256].astype(BF16)

    for i in range(4):
        d = (y - 1 - r + i + 8) % 8
        yt = d // 4
        fi = (d % 4) // 2
        keys = kv[yt]
        q = q_all[:, 32 * i : 32 * i + 32, :].reshape(128, 256)
        scale = bias[yt, 2]
        s = dot_t(q, keys) * scale + bias[yt, fi]
        top = jnp.max(s, axis=1, keepdims=True)
        expo = jnp.exp(s - top)
        norm = jnp.sum(expo, axis=1, keepdims=True)
        u = dot((expo * scale).astype(BF16), keys) / norm
        u_all[:, 32 * i : 32 * i + 32, :] = u.reshape(4, 32, 256)

    pltpu.make_async_remote_copy(
        fv_all.at[1 - r], fv_all.at[1 - r], sp.at[2], rp.at[2], partner, MESH
    ).wait_recv()
    for role in range(2):
        for h in range(2):
            hi, lo = split2(u_all[2 * role + h])
            cols = slice(HS * h, HS * h + HS)
            v_hi = fv_all[role, 0, :, cols]
            v_lo = fv_all[role, 1, :, cols]
            a = dot(hi, v_hi) + dot(lo, v_hi) + dot(hi, v_lo)
            a_all[:, 256 * role + HS * h : 256 * role + HS * h + HS] = a.astype(BF16)

    pltpu.make_async_remote_copy(
        wo.at[1 - r], wo.at[1 - r], sp.at[0], rp.at[0], partner, MESH
    ).wait_recv()
    width = 3072 // CHUNKS
    own_i = 1 + r

    def copy_c(c, step):
        i = (own_i + step) % 4
        d = (y - 1 - r + i + 8) % 8
        return pltpu.make_async_remote_copy(
            send_c.at[c, i], recv_c.at[c, i], sc.at[c, step], rc.at[c, i], ring(d, r), MESH
        )

    def land_c(c, step):
        i = (own_i + step) % 4
        d = (y + 1 + r - i + 8) % 8
        return pltpu.make_async_remote_copy(
            send_c.at[c, i], recv_c.at[c, i], sc.at[c, step], rc.at[c, i], ring(d, r), MESH
        )

    for c in range(CHUNKS):
        cols = slice(width * c, width * c + width)
        part = dot(a_all[:, 0:256], wo[0, :, cols]) + dot(a_all[:, 256:512], wo[1, :, cols])
        part = part.reshape(4, 32, width)
        acc[c] = part
        send_c[c] = part.astype(BF16)
        for step in range(1, 4):
            copy_c(c, step).start()

    own_lat = lat_q[pl.ds(pl.multiple_of(own_i * 32, 32), 32), :]
    own_patch = pl.multiple_of(((m % 2) * 2 + r) * 32, 32)
    for c in range(CHUNKS):
        cols = slice(width * c, width * c + width)
        embedded = dot(own_lat, e[:, cols]) + pos[pl.ds(own_patch, 32), cols].astype(F32)
        acc[c, own_i] = acc[c, own_i] + embedded
    for c in range(CHUNKS):
        cols = slice(width * c, width * c + width)
        total = acc[c, own_i]
        for step in range(1, 4):
            land_c(c, step).wait_recv()
            total = total + recv_c[c, (own_i + step) % 4].astype(F32)
        out_ref[:, cols] = total.astype(BF16)

    for step in range(1, 8):
        copy_a(step).wait_send()
        copy_x(step).wait_send()
        copy_z(step).wait_send()

    @pl.when(jnp.logical_not(is_self))
    def _():
        copy_z(0).wait_send()

    for idx in range(8):
        forward(idx).wait_send()
    wo_copy.wait_send()
    m_copy.wait_send()
    f_copy.wait_send()
    for c in range(CHUNKS):
        for step in range(1, 4):
            copy_c(c, step).wait_send()


def on_device(
    gen_hidden,
    gen_out_weight,
    patch_order,
    frame_block,
    embed_weight,
    pos_table,
    norm_gain,
    qkv_weight,
    out_weight,
):
    any_space = pl.BlockSpec(memory_space=pl.ANY)
    vmem = pl.BlockSpec(memory_space=pltpu.VMEM)
    smem = pl.BlockSpec(memory_space=pltpu.SMEM)
    dma = pltpu.SemaphoreType.DMA
    width = 3072 // CHUNKS
    scratch = [
        pltpu.VMEM((256, 384), BF16),
        pltpu.VMEM((384, 128), BF16),
        pltpu.VMEM((128, 3072), BF16),
        pltpu.VMEM((128, 3072), BF16),
        pltpu.VMEM((3, 3072, 256), BF16),
        pltpu.VMEM((2, 256, 3072), BF16),
        pltpu.VMEM((288, 128), F32),
        pltpu.VMEM((8, 48, 128), F32),
        pltpu.VMEM((8, 48, 128), F32),
        pltpu.VMEM((8, 16, 128), BF16),
        pltpu.VMEM((8, 16, 128), BF16),
        pltpu.VMEM((2, 64, 128), BF16),
        pltpu.VMEM((2, 16, 64, 128), BF16),
        pltpu.VMEM((2, 1024, 256), BF16),
        pltpu.VMEM((512, 3072), BF16),
        pltpu.VMEM((2, 2, 256, 512), BF16),
        pltpu.VMEM((2, 2, 256, 256), BF16),
        pltpu.VMEM((4, 32, 1024), BF16),
        pltpu.VMEM((1024, 128), F32),
        pltpu.VMEM((128, 128), F32),
        pltpu.VMEM((128, 128), F32),
        pltpu.VMEM((1, 1024), F32),
        pltpu.VMEM((2, 3, 1, 1024), F32),
        pltpu.VMEM((128, 256), BF16),
        pltpu.VMEM((128, 128), BF16),
        pltpu.VMEM((4, 128, 256), BF16),
        pltpu.VMEM((4, 128, 256), F32),
        pltpu.VMEM((128, 512), BF16),
        pltpu.VMEM((CHUNKS, 4, 32, width), F32),
        pltpu.VMEM((CHUNKS, 4, 32, width), BF16),
        pltpu.VMEM((CHUNKS, 4, 32, width), BF16),
        dma((6,)),
        dma((8,)),
        dma((8,)),
        dma((8,)),
        dma((8,)),
        dma((8,)),
        dma((8,)),
        dma((8,)),
        dma((8,)),
        dma((3,)),
        dma((3,)),
        dma((CHUNKS, 4)),
        dma((CHUNKS, 4)),
    ]
    return pl.pallas_call(
        kernel,
        out_shape=jax.ShapeDtypeStruct((32, 3072), BF16),
        in_specs=[
            any_space,
            any_space,
            vmem,
            smem,
            any_space,
            any_space,
            vmem,
            any_space,
            any_space,
        ],
        out_specs=vmem,
        scratch_shapes=scratch,
        compiler_params=pltpu.CompilerParams(collective_id=0, has_side_effects=True),
    )(
        gen_hidden.reshape(256, 384),
        gen_out_weight,
        patch_order.reshape(1, 128),
        frame_block,
        embed_weight,
        pos_table,
        norm_gain.reshape(1, 3072),
        jnp.transpose(qkv_weight, (1, 0, 2)),
        out_weight,
    )


def solution(mesh):
    in_specs = (
        P("seq", None, ("mp", "role")),
        P(("mp", "role"), None),
        P(),
        P(),
        P(),
        P(),
        P(),
        P(None, None, ("mp", "role")),
        P(("mp", "role"), None),
    )
    out_specs = P(("seq", "mp", "role"), None)
    return jax.shard_map(
        on_device, mesh=mesh, in_specs=in_specs, out_specs=out_specs, check_vma=False
    )
```

time: 171 us -> 65.8 us (0.38)
  the two profiles are of different devices: /device:TPU:112 before, /device:TPU:1 now
where the time goes in v1:
time: 65.8 us; the launch traced here: 65.5 us
  Pallas kernels  62.6 us (95%)
  local copies, waits for them, and re-layouts  2.91 us (4%)
    pallas_call x1, Pallas kernels, on_device(): pl.pallas_call(kernel, out_shape=jax.ShapeDtypeStruct((32, 3072), BF16),...  62.6 us
    unnamed x1, local copies, waits for them, and re-layouts  1.62 us

profile of v1, /device:TPU:1, one launch (start us, length us, event | category | flops | bytes accessed | tf_op | source)
XLA Modules:
  0.0 65.5 jit_solution(4852387415821059876)
XLA Ops:
  0.0 1.3 %reshape.11.gain_ref = bf16[1,3072]{1,0:T(2,128)(2,1)} reshape(bf16[3072]{0:T(1024)(128)(2,1)} %param.15) | data formatting | bytes 12288 | tf_op jit(solution)/shard_map/reshape | solution.py:562
  1.3 62.6 %shard_map.91 = bf16[32,3072]{1,0:T(8,128)(2,1)} custom-call(bf16[256,384]{1,0:T(8,128)(2,1)} %bitcast.4, bf16[384,128]{1,0:T(8,128)(2,1)} %gw_hbm.1, s32[1,128]{1,0:T(1,128)} %bitcast.5, s32[256]{0:T(256)} %fb_ref.1, bf16[128,3072]{1,0:T(8,128)(2,1)} %e_hbm.1, bf16[128,3072]{1,0:T(8,128)(2,1)} %pos_hbm.1, bf16[1,3072]{1,0:T(2,128)(2,1)} %reshape.11.gain_ref, ...), custom_call_target="tpu_custom_call" | custom-call | tf_op jit(solution)/shard_map/pallas_call | solution.py:538
  63.9 1.6 %copy.11 = bf16[32,3072]{1,0:T(8,128)(2,1)} copy(bf16[32,3072]{1,0:T(8,128)(2,1)} %shard_map.91) | data formatting | bytes 393216

commit v2 on v1

v2 whole, which is shorter than its diff:
```python
import functools

import jax
import jax.numpy as jnp
from jax import lax
from jax.experimental import pallas as pl
from jax.experimental.pallas import tpu as pltpu
from jax.sharding import PartitionSpec as P

MESH = pl.DeviceIdType.MESH
F32 = jnp.float32
BF16 = jnp.bfloat16
HS = 128
CHUNKS = 4
NEG = -1e30


def dot(a, b, precision=None):
    return jnp.dot(a, b, preferred_element_type=F32, precision=precision)


def dot_t(a, b, precision=None):
    return lax.dot_general(
        a, b, (((1,), (1,)), ((), ())), preferred_element_type=F32, precision=precision
    )


def split2(a):
    hi = a.astype(BF16)
    return hi, (a - hi.astype(F32)).astype(BF16)


def iota(shape, dim):
    return lax.broadcasted_iota(jnp.int32, shape, dim)


def slot_of(row):
    part = lax.shift_right_logical(row, 3)
    parity = lax.shift_right_logical(part, 6)
    half = jnp.bitwise_and(lax.shift_right_logical(part, 5), 1)
    rest = jnp.bitwise_and(lax.shift_right_logical(part, 3), 3)
    return half * 64 + rest * 16 + parity * 8 + jnp.bitwise_and(part, 7)


def kernel(
    gh_hbm,
    gw_hbm,
    po_hbm,
    fb_hbm,
    e_hbm,
    pos_hbm,
    gain_hbm,
    w_hbm,
    wo_hbm,
    out_hbm,
    gh,
    gw,
    po_ref,
    fb_ref,
    gain_ref,
    out_ref,
    e,
    pos,
    w,
    wo,
    ppad,
    send_a,
    recv_a,
    send_x,
    recv_x,
    send_z,
    lat,
    kv,
    fhl,
    m_all,
    fv_all,
    sel_q,
    hr2,
    he2,
    ncol,
    nlane,
    bias,
    key_scale,
    gg,
    lat_q,
    q_all,
    u_all,
    a_all,
    acc,
    send_c,
    recv_c,
    load_sem,
    out_sem,
    sa,
    ra,
    sx,
    rx,
    sz,
    rz,
    sf,
    rf,
    sp,
    rp,
    sc,
    rc,
):
    seq = lax.axis_index("seq")
    m = lax.axis_index("mp")
    r = lax.axis_index("role")
    ys = seq // 64
    z = (seq // 8) % 8
    x = seq % 8
    j = 2 * m + r
    y = ys * 4 + m
    is_self = jnp.logical_and(j == z, True)

    def group(k):
        return (seq, k // 2, k % 2)

    def row_x(x2):
        return (ys * 64 + z * 8 + x2, m, r)

    def ring(y2, role):
        return ((y2 // 4) * 64 + z * 8 + x, y2 % 4, role)

    def zy_source(idx):
        return ((idx // 4) * 64 + (2 * (idx % 4) + r) * 8 + x, z // 2, z % 2)

    def zy_dest(i):
        y2 = (y + i) % 8
        return ((y2 // 4) * 64 + j * 8 + x, y2 % 4, z % 2)

    def place_of(p):
        first = 2 * (1 - r) if p < 2 else 2 * r
        return (y - 1 - r + first + p % 2 + 8) % 8

    def source_of(p):
        first = 2 * (1 - r) if p < 2 else 2 * r
        return (y + 1 + r - first - p % 2 + 8) % 8

    partner = (seq, m, 1 - r)

    def load(src, dst, n):
        return pltpu.make_async_copy(src, dst, load_sem.at[n])

    load_gh = load(gh_hbm, gh, 0)
    load_gw = load(gw_hbm, gw, 1)
    load_po = load(po_hbm, po_ref, 2)
    load_fb = load(fb_hbm, fb_ref, 3)
    load_gain = load(gain_hbm, gain_ref, 4)
    load_e = load(e_hbm, e, 5)
    load_pos = load(pos_hbm, pos, 6)
    load_w = load(w_hbm, w, 7)
    load_wo = load(wo_hbm, wo.at[r], 8)
    for copy in (load_gh, load_gw, load_po, load_fb, load_gain):
        copy.start()

    barrier = pltpu.get_barrier_semaphore()

    def greet(device):
        pl.semaphore_signal(barrier, inc=1, device_id=device, device_id_type=MESH)

    for step in range(1, 8):
        greet(group((j + step) % 8))
        greet(row_x((x + step) % 8))
    for idx in range(8):
        here = jnp.logical_and(is_self, idx == ys * 4 + z // 2)

        @pl.when(jnp.logical_not(here))
        def _():
            greet(zy_source(idx))

    for step in range(1, 4):
        i = (1 + r + step) % 4
        greet(ring((y + 1 + r - i + 8) % 8, r))

    ppad[0:8, :] = jnp.zeros((8, 128), F32)
    ppad[264:288, :] = jnp.zeros((24, 128), F32)

    load_gh.wait()
    load_gw.wait()
    ppad[8:264, :] = dot(gh[...], gw[...])
    for k in range(8):
        for yt in range(2):
            first = 128 * yt + 16 * k + 5
            send_a[k, 24 * yt : 24 * yt + 24, :] = ppad[first : first + 24, :]

    pl.semaphore_wait(barrier, 25 - is_self.astype(jnp.int32))

    def copy_a(step):
        k = (j + step) % 8
        return pltpu.make_async_remote_copy(
            send_a.at[k], recv_a.at[j], sa.at[step], ra.at[j], group(k), MESH
        )

    def land_a(step):
        k = (j + step) % 8
        return pltpu.make_async_remote_copy(
            send_a.at[k], recv_a.at[k], sa.at[step], ra.at[k], group(k), MESH
        )

    for step in range(1, 8):
        copy_a(step).start()
    for copy in (load_e, load_pos, load_w, load_wo):
        copy.start()

    load_po.wait()
    load_fb.wait()
    po_f = jnp.broadcast_to(po_ref[...], (16, 128)).astype(F32).astype(BF16)
    spread = (iota((128, 1024), 0) == slot_of(iota((128, 1024), 1))).astype(F32).astype(BF16)
    po_lane = dot(po_f, spread)[0:1]
    perm_t = (jnp.broadcast_to(po_ref[...], (128, 128)) == iota((128, 128), 0)).astype(F32).astype(
        BF16
    )
    rows8 = (slot_of(iota((1024, 128), 0)) == iota((1024, 128), 1)).astype(F32).astype(BF16)
    onehot = dot_t(rows8, perm_t).astype(BF16)
    kv[0, :, 128:256] = onehot
    kv[1, :, 128:256] = onehot
    w_lane = jnp.bitwise_and(iota((1, 1024), 1), 7)
    for yt in range(2):
        base = yt * 128 + z * 16 + x * 2 - 3
        blocks = []
        key_block = jnp.full((1, 1024), -1, jnp.int32)
        for n in range(8):
            frame = base + n
            value = fb_ref[jnp.clip(frame, 0, 255)]
            value = jnp.where(jnp.logical_and(frame >= 0, frame <= 255), value, -1)
            blocks.append(value)
            key_block = jnp.where(w_lane == n, value, key_block)
        for fi in range(2):
            bias[yt, fi] = jnp.where(key_block == blocks[3 + fi], F32(0), F32(NEG))
    for p in range(4):
        d = place_of(p)
        fi = (d % 4) // 2
        patch = ((d % 2) * 2 + r) * 32
        rows = (iota((32, 1024), 0) + patch).astype(F32)
        hit = jnp.logical_and(
            jnp.broadcast_to(po_lane, (32, 1024)) == rows,
            jnp.broadcast_to(w_lane, (32, 1024)) == 3 + fi,
        )
        sel_q[p] = hit.astype(F32).astype(BF16)

    load_e.wait()
    load_pos.wait()
    load_gain.wait()
    gain = gain_ref[...].astype(F32)
    for n, table in enumerate((e, pos)):
        for part in range(24):
            cols = slice(128 * part, 128 * part + 128)
            hi, lo = split2(table[:, cols].astype(F32) * gain[part : part + 1, :])
            fhl[n * 128 : n * 128 + 128, cols] = hi
            fhl[256 + n * 128 : 384 + n * 128, cols] = lo
    ghi, glo = split2(dot_t(e[...], e[...]))
    gg[:, 0:128] = ghi
    gg[:, 128:256] = glo
    he = 2.0 * dot_t(pos[...], e[...])
    he2[...] = he
    he_hi, he_lo = split2(he)
    hr2[...] = dot(onehot, he_hi) + dot(onehot, he_lo)
    norms = dot_t(pos[...], pos[...])
    diagonal = jnp.where(iota((128, 128), 0) == iota((128, 128), 1), norms, F32(0))
    ncol[...] = jnp.broadcast_to(jnp.sum(diagonal, axis=1, keepdims=True), (128, 128))
    nrow = jnp.broadcast_to(jnp.sum(diagonal, axis=0, keepdims=True), (8, 128))
    norm_lane = dot_t(nrow, onehot.astype(F32), lax.Precision.HIGHEST)[0:1]
    for n in range(4):
        nlane[n] = norm_lane[:, 256 * n : 256 * n + 256]
    load_w.wait()
    load_wo.wait()
    wo_copy = pltpu.make_async_remote_copy(
        wo.at[r], wo.at[r], sp.at[0], rp.at[0], partner, MESH
    )
    wo_copy.start()

    def weight_product(c):
        both = dot(fhl[...], w[c])
        return both[0:256] + both[256:512]

    for step in range(1, 8):
        land_a(step).wait_recv()
    total = send_a[j]
    for step in range(1, 8):
        total = total + recv_a[(j + step) % 8]
    recv_a[j] = total
    for n in range(8):
        halves = [recv_a[j, 24 * yt + 2 * n : 24 * yt + 2 * n + 8, :] for yt in range(2)]
        send_x[n] = jnp.concatenate(halves, axis=0).astype(BF16)

    def copy_x(step):
        x2 = (x + step) % 8
        return pltpu.make_async_remote_copy(
            send_x.at[x2], recv_x.at[x], sx.at[step], rx.at[x], row_x(x2), MESH
        )

    def land_x(step):
        x2 = (x + step) % 8
        return pltpu.make_async_remote_copy(
            send_x.at[x2], recv_x.at[x2], sx.at[step], rx.at[x2], row_x(x2), MESH
        )

    for step in range(1, 8):
        copy_x(step).start()
    recv_x[x] = send_x[x]

    fq = weight_product(0)
    fk = weight_product(1)

    for step in range(1, 8):
        land_x(step).wait_recv()
    for a in range(4):
        first = recv_x[2 * a].astype(F32)
        second = recv_x[2 * a + 1].astype(F32)
        for yt in range(2):
            pair = jnp.concatenate(
                [first[8 * yt : 8 * yt + 8], second[8 * yt : 8 * yt + 8]], axis=0
            )
            send_z[yt, 16 * a : 16 * a + 16, :] = pair.astype(BF16)

    half = z % 2
    own_idx = ys * 4 + z // 2

    def copy_z(i):
        return pltpu.make_async_remote_copy(
            send_z, lat.at[:, half, own_idx], sz.at[i], rz.at[own_idx], zy_dest(i), MESH
        )

    local_z = pltpu.make_async_copy(send_z, lat.at[:, half, own_idx], rz.at[own_idx])
    for i in range(1, 8):
        copy_z(i).start()

    @pl.when(jnp.logical_not(is_self))
    def _():
        copy_z(0).start()

    @pl.when(is_self)
    def _():
        local_z.start()

    for h in range(2):
        cols = slice(HS * h, HS * h + HS)
        bil = dot_t(fq[:, cols], fk[:, cols], lax.Precision.HIGHEST)
        hi, lo = split2(bil)
        m_all[r, 0, :, 256 * h : 256 * h + 256] = hi
        m_all[r, 1, :, 256 * h : 256 * h + 256] = lo
    hi, lo = split2(weight_product(2))
    fv_all[r, 0] = hi
    fv_all[r, 1] = lo
    m_copy = pltpu.make_async_remote_copy(
        m_all.at[r], m_all.at[r], sp.at[1], rp.at[1], partner, MESH
    )
    f_copy = pltpu.make_async_remote_copy(
        fv_all.at[r], fv_all.at[r], sp.at[2], rp.at[2], partner, MESH
    )
    m_copy.start()
    f_copy.start()

    def forward(idx):
        block = lat.at[:, r, idx]
        return pltpu.make_async_remote_copy(
            block, block, sf.at[idx], rf.at[idx], partner, MESH
        )

    def forwarded(idx):
        block = lat.at[:, 1 - r, idx]
        return pltpu.make_async_remote_copy(
            block, block, sf.at[idx], rf.at[idx], partner, MESH
        )

    ones = jnp.ones((8, 128), F32)

    def take_batch(parity, n):
        batch = parity * 2 + n
        first = pl.multiple_of(batch * 256, 256)
        for yt in range(2):
            rows = lat[yt, parity, 4 * n : 4 * n + 4].reshape(256, 128)
            kv[yt, pl.ds(first, 256), 0:128] = rows
            both = dot(rows, gg[...])
            cross = both[:, 0:128] + both[:, 128:256] + hr2[pl.ds(first, 256), :]
            total = dot_t(ones, rows.astype(F32) * cross, lax.Precision.HIGHEST)[0:1]
            total = total + nlane[batch]
            key_scale[yt, batch] = lax.rsqrt(
                jnp.maximum(total, 0.0) * F32(1 / 3072) + F32(1e-06)
            )

    for n in range(2):
        for idx in range(4 * n, 4 * n + 4):
            block = lat.at[:, r, idx]
            pltpu.make_async_copy(block, block, rz.at[idx]).wait()
            forward(idx).start()
        take_batch(r, n)
    for n in range(2):
        for idx in range(4 * n, 4 * n + 4):
            forwarded(idx).wait_recv()
        take_batch(1 - r, n)

    tokens = []
    scales = []
    for p in range(4):
        d = place_of(p)
        patch = pl.multiple_of(((d % 2) * 2 + r) * 32, 32)
        mine = dot(sel_q[p], kv[d // 4, :, 0:128])
        lat_q[32 * p : 32 * p + 32, :] = mine.astype(BF16)
        both = dot(mine.astype(BF16), gg[...])
        squares = mine * (both[:, 0:128] + both[:, 128:256] + he2[pl.ds(patch, 32), :])
        total = jnp.sum(squares, axis=1, keepdims=True) + ncol[pl.ds(patch, 32), 0:1]
        scales.append(
            lax.rsqrt(jnp.maximum(total, 0.0) * F32(1 / 3072) + F32(1e-06))
            * F32(1 / HS**0.5)
        )
        place = (iota((32, 128), 0) + patch == iota((32, 128), 1)).astype(F32).astype(BF16)
        tokens.append(jnp.concatenate([mine.astype(BF16), place], axis=1))
    tokens = jnp.concatenate(tokens, axis=0)
    scales = jnp.concatenate(scales, axis=0)
    pltpu.make_async_remote_copy(
        m_all.at[1 - r], m_all.at[1 - r], sp.at[1], rp.at[1], partner, MESH
    ).wait_recv()
    for role in range(2):
        q = (dot(tokens, m_all[role, 0]) + dot(tokens, m_all[role, 1])) * scales
        for h in range(2):
            q_all[2 * role + h] = q[:, 256 * h : 256 * h + 256].astype(BF16)

    width = 3072 // CHUNKS

    def copy_c(c, p):
        return pltpu.make_async_remote_copy(
            send_c.at[c, p], recv_c.at[c, p], sc.at[c, p], rc.at[c, p], ring(place_of(p), r), MESH
        )

    def land_c(c, p):
        return pltpu.make_async_remote_copy(
            send_c.at[c, p], recv_c.at[c, p], sc.at[c, p], rc.at[c, p], ring(source_of(p), r), MESH
        )

    near = 2 + r

    def copy_near(c):
        d = (y + 1 - 2 * (1 - r) + 8) % 8
        return pltpu.make_async_remote_copy(
            send_c.at[c, near],
            recv_c.at[c, near],
            sc.at[c, near],
            rc.at[c, near],
            ring(d, r),
            MESH,
        )

    def land_near(c):
        d = (y - 1 + 2 * (1 - r) + 8) % 8
        return pltpu.make_async_remote_copy(
            send_c.at[c, near],
            recv_c.at[c, near],
            sc.at[c, near],
            rc.at[c, near],
            ring(d, r),
            MESH,
        )

    for g in range(2):
        for p in (2 * g, 2 * g + 1):
            d = place_of(p)
            yt = d // 4
            fi = (d % 4) // 2
            keys = kv[yt]
            q = q_all[:, 32 * p : 32 * p + 32, :].reshape(128, 256)
            scale = jnp.concatenate([key_scale[yt, n] for n in range(4)], axis=1)
            s = dot_t(q, keys) * scale + bias[yt, fi]
            top = jnp.max(s, axis=1, keepdims=True)
            expo = jnp.exp(s - top)
            norm = jnp.sum(expo, axis=1, keepdims=True)
            u = dot((expo * scale).astype(BF16), keys) / norm
            u_all[:, 32 * p : 32 * p + 32, :] = u.reshape(4, 32, 256)
        if g == 0:
            pltpu.make_async_remote_copy(
                fv_all.at[1 - r], fv_all.at[1 - r], sp.at[2], rp.at[2], partner, MESH
            ).wait_recv()
            pltpu.make_async_remote_copy(
                wo.at[1 - r], wo.at[1 - r], sp.at[0], rp.at[0], partner, MESH
            ).wait_recv()
        rows = slice(64 * g, 64 * g + 64)
        for role in range(2):
            for h in range(2):
                hi, lo = split2(u_all[2 * role + h, rows, :])
                cols = slice(HS * h, HS * h + HS)
                v_hi = fv_all[role, 0, :, cols]
                v_lo = fv_all[role, 1, :, cols]
                a = dot(hi, v_hi) + dot(lo, v_hi) + dot(hi, v_lo)
                a_all[rows, 256 * role + HS * h : 256 * role + HS * h + HS] = a.astype(BF16)
        for c in range(CHUNKS):
            cols = slice(width * c, width * c + width)
            part = dot(a_all[rows, 0:256], wo[0, :, cols]) + dot(
                a_all[rows, 256:512], wo[1, :, cols]
            )
            part = part.reshape(2, 32, width)
            send_c[c, 2 * g : 2 * g + 2] = part.astype(BF16)
            if g == 0:
                copy_c(c, 0).start()
                copy_c(c, 1).start()
            else:
                acc[c] = part
                copy_near(c).start()

    own_lat = lat_q[pl.ds(pl.multiple_of((3 - r) * 32, 32), 32), :]
    own_patch = pl.multiple_of(((m % 2) * 2 + r) * 32, 32)
    for c in range(CHUNKS):
        cols = slice(width * c, width * c + width)
        embedded = dot(own_lat, e[:, cols]) + pos[pl.ds(own_patch, 32), cols].astype(F32)
        acc[c, 1 - r] = acc[c, 1 - r] + embedded
    outs = []
    for c in range(CHUNKS):
        cols = slice(width * c, width * c + width)
        land_c(c, 0).wait_recv()
        land_c(c, 1).wait_recv()
        land_near(c).wait_recv()
        total = acc[c, 1 - r] + recv_c[c, 0].astype(F32)
        total = total + recv_c[c, 1].astype(F32)
        total = total + recv_c[c, near].astype(F32)
        out_ref[:, cols] = total.astype(BF16)
        outs.append(
            pltpu.make_async_copy(out_ref.at[:, cols], out_hbm.at[:, cols], out_sem.at[c])
        )
        outs[-1].start()

    for step in range(1, 8):
        copy_a(step).wait_send()
        copy_x(step).wait_send()
        copy_z(step).wait_send()

    @pl.when(jnp.logical_not(is_self))
    def _():
        copy_z(0).wait_send()

    for idx in range(8):
        forward(idx).wait_send()
    wo_copy.wait_send()
    m_copy.wait_send()
    f_copy.wait_send()
    for c in range(CHUNKS):
        copy_c(c, 0).wait_send()
        copy_c(c, 1).wait_send()
        copy_near(c).wait_send()
    for copy in outs:
        copy.wait()


def on_device(
    gen_hidden,
    gen_out_weight,
    patch_order,
    frame_block,
    embed_weight,
    pos_table,
    norm_gain,
    qkv_weight,
    out_weight,
):
    any_space = pl.BlockSpec(memory_space=pl.ANY)
    dma = pltpu.SemaphoreType.DMA
    width = 3072 // CHUNKS
    scratch = [
        pltpu.VMEM((256, 384), BF16),
        pltpu.VMEM((384, 128), BF16),
        pltpu.VMEM((1, 128), jnp.int32),
        pltpu.SMEM((256,), jnp.int32),
        pltpu.VMEM((24, 128), BF16),
        pltpu.VMEM((32, 3072), BF16),
        pltpu.VMEM((128, 3072), BF16),
        pltpu.VMEM((128, 3072), BF16),
        pltpu.VMEM((3, 3072, 256), BF16),
        pltpu.VMEM((2, 256, 3072), BF16),
        pltpu.VMEM((288, 128), F32),
        pltpu.VMEM((8, 48, 128), F32),
        pltpu.VMEM((8, 48, 128), F32),
        pltpu.VMEM((8, 16, 128), BF16),
        pltpu.VMEM((8, 16, 128), BF16),
        pltpu.VMEM((2, 64, 128), BF16),
        pltpu.VMEM((2, 2, 8, 64, 128), BF16),
        pltpu.VMEM((2, 1024, 256), BF16),
        pltpu.VMEM((512, 3072), BF16),
        pltpu.VMEM((2, 2, 256, 512), BF16),
        pltpu.VMEM((2, 2, 256, 256), BF16),
        pltpu.VMEM((4, 32, 1024), BF16),
        pltpu.VMEM((1024, 128), F32),
        pltpu.VMEM((128, 128), F32),
        pltpu.VMEM((128, 128), F32),
        pltpu.VMEM((4, 1, 256), F32),
        pltpu.VMEM((2, 2, 1, 1024), F32),
        pltpu.VMEM((2, 4, 1, 256), F32),
        pltpu.VMEM((128, 256), BF16),
        pltpu.VMEM((128, 128), BF16),
        pltpu.VMEM((4, 128, 256), BF16),
        pltpu.VMEM((4, 128, 256), F32),
        pltpu.VMEM((128, 512), BF16),
        pltpu.VMEM((CHUNKS, 2, 32, width), F32),
        pltpu.VMEM((CHUNKS, 4, 32, width), BF16),
        pltpu.VMEM((CHUNKS, 4, 32, width), BF16),
        dma((9,)),
        dma((CHUNKS,)),
        dma((8,)),
        dma((8,)),
        dma((8,)),
        dma((8,)),
        dma((8,)),
        dma((8,)),
        dma((8,)),
        dma((8,)),
        dma((3,)),
        dma((3,)),
        dma((CHUNKS, 4)),
        dma((CHUNKS, 4)),
    ]
    return pl.pallas_call(
        kernel,
        out_shape=jax.ShapeDtypeStruct((32, 3072), BF16),
        in_specs=[any_space] * 9,
        out_specs=any_space,
        scratch_shapes=scratch,
        compiler_params=pltpu.CompilerParams(collective_id=0, has_side_effects=True),
    )(
        gen_hidden.reshape(256, 384),
        gen_out_weight,
        patch_order.reshape(1, 128),
        frame_block,
        embed_weight,
        pos_table,
        norm_gain.reshape(24, 128),
        jnp.transpose(qkv_weight, (1, 0, 2)),
        out_weight,
    )


def solution(mesh):
    in_specs = (
        P("seq", None, ("mp", "role")),
        P(("mp", "role"), None),
        P(),
        P(),
        P(),
        P(),
        P(),
        P(None, None, ("mp", "role")),
        P(("mp", "role"), None),
    )
    out_specs = P(("seq", "mp", "role"), None)
    return jax.shard_map(
        on_device, mesh=mesh, in_specs=in_specs, out_specs=out_specs, check_vma=False
    )
```

time: 65.8 us -> 62.8 us (0.954)
  Pallas kernels: 62.6 us -> 60.8 us
  local copies, waits for them, and re-layouts: 2.91 us -> 1.62 us
    pallas_call x1, Pallas kernels: 62.6 us -> 60.8 us  [on_device(): pl.pallas_call(kernel, out_shape=jax.ShapeDtypeStruct((32, 3072), BF16),...]
    reshape x1 -> x0, local copies, waits for them, and re-layouts: 1.3 us -> none  [on_device(): norm_gain.reshape(1, 3072)]
where the time goes in v2:
time: 62.8 us; the launch traced here: 62.4 us
  Pallas kernels  60.8 us (97%)
  local copies, waits for them, and re-layouts  1.62 us (3%)
    pallas_call x1, Pallas kernels, on_device(): pl.pallas_call(kernel, out_shape=jax.ShapeDtypeStruct((32, 3072), BF16),...  60.8 us
    unnamed x1, local copies, waits for them, and re-layouts  1.62 us

profile of v2, /device:TPU:1, one launch (start us, length us, event | category | flops | bytes accessed | tf_op | source)
XLA Modules:
  0.0 62.4 jit_solution(1592943372609003942)
XLA Ops:
  0.0 60.8 %shard_map.91 = bf16[32,3072]{1,0:T(8,128)(2,1)} custom-call(bf16[256,384]{1,0:T(8,128)(2,1)} %bitcast.5, bf16[384,128]{1,0:T(8,128)(2,1)} %gw_hbm.1, s32[1,128]{1,0:T(1,128)} %bitcast.7, s32[256]{0:T(256)} %fb_hbm.1, bf16[128,3072]{1,0:T(8,128)(2,1)} %e_hbm.1, bf16[128,3072]{1,0:T(8,128)(2,1)} %pos_hbm.1, bf16[24,128]{1,0:T(8,128)(2,1)} %bitcast.6, ...), custom_call_target="tpu_custom_call" | custom-call | tf_op jit(solution)/shard_map/pallas_call | solution.py:610
  60.8 1.6 %copy.11 = bf16[32,3072]{1,0:T(8,128)(2,1)} copy(bf16[32,3072]{1,0:T(8,128)(2,1)} %shard_map.91) | data formatting | bytes 393216

commit v3 on v2

--- a/solution.py
+++ b/solution.py
@@ -64,6 +64,7 @@
     w,
     wo,
     ppad,
+    mine,
     send_a,
     recv_a,
     send_x,
@@ -130,13 +131,14 @@
         y2 = (y + i) % 8
         return ((y2 // 4) * 64 + j * 8 + x, y2 % 4, z % 2)
 
+    side = 1 - 2 * r
+    offsets = (2, -1, 1, 0)
+
     def place_of(p):
-        first = 2 * (1 - r) if p < 2 else 2 * r
-        return (y - 1 - r + first + p % 2 + 8) % 8
+        return (y + side * offsets[p] + 8) % 8
 
     def source_of(p):
-        first = 2 * (1 - r) if p < 2 else 2 * r
-        return (y + 1 + r - first - p % 2 + 8) % 8
+        return (y - side * offsets[p] + 8) % 8
 
     partner = (seq, m, 1 - r)
 
@@ -152,17 +154,14 @@
     load_pos = load(pos_hbm, pos, 6)
     load_w = load(w_hbm, w, 7)
     load_wo = load(wo_hbm, wo.at[r], 8)
-    for copy in (load_gh, load_gw, load_po, load_fb, load_gain):
-        copy.start()
+    load_gh.start()
+    load_gw.start()
 
     barrier = pltpu.get_barrier_semaphore()
 
     def greet(device):
         pl.semaphore_signal(barrier, inc=1, device_id=device, device_id_type=MESH)
 
-    for step in range(1, 8):
-        greet(group((j + step) % 8))
-        greet(row_x((x + step) % 8))
     for idx in range(8):
         here = jnp.logical_and(is_self, idx == ys * 4 + z // 2)
 
@@ -170,10 +169,15 @@
         def _():
             greet(zy_source(idx))
 
-    for step in range(1, 4):
-        i = (1 + r + step) % 4
-        greet(ring((y + 1 + r - i + 8) % 8, r))
-
+    for step in range(1, 8):
+        greet(row_x((x + step) % 8))
+    for step in range(1, 8):
+        greet(group((j + step) % 8))
+    for p in range(3):
+        greet(ring(source_of(p), r))
+
+    for copy in (load_po, load_fb, load_gain):
+        copy.start()
     ppad[0:8, :] = jnp.zeros((8, 128), F32)
     ppad[264:288, :] = jnp.zeros((24, 128), F32)
 
@@ -181,9 +185,10 @@
     load_gw.wait()
     ppad[8:264, :] = dot(gh[...], gw[...])
     for k in range(8):
-        for yt in range(2):
-            first = 128 * yt + 16 * k + 5
-            send_a[k, 24 * yt : 24 * yt + 24, :] = ppad[first : first + 24, :]
+        parts = [ppad[128 * yt + 16 * k + 5 : 128 * yt + 16 * k + 29, :] for yt in range(2)]
+        part = jnp.concatenate(parts, axis=0)
+        mine[k] = part
+        send_a[k] = part.astype(BF16)
 
     pl.semaphore_wait(barrier, 25 - is_self.astype(jnp.int32))
 
@@ -203,6 +208,10 @@
         copy_a(step).start()
     for copy in (load_e, load_pos, load_w, load_wo):
         copy.start()
+    wo_copy = pltpu.make_async_remote_copy(
+        wo_hbm, wo.at[r], sp.at[0], rp.at[0], partner, MESH
+    )
+    wo_copy.start()
 
     load_po.wait()
     load_fb.wait()
@@ -266,10 +275,6 @@
         nlane[n] = norm_lane[:, 256 * n : 256 * n + 256]
     load_w.wait()
     load_wo.wait()
-    wo_copy = pltpu.make_async_remote_copy(
-        wo.at[r], wo.at[r], sp.at[0], rp.at[0], partner, MESH
-    )
-    wo_copy.start()
 
     def weight_product(c):
         both = dot(fhl[...], w[c])
@@ -277,12 +282,12 @@
 
     for step in range(1, 8):
         land_a(step).wait_recv()
-    total = send_a[j]
-    for step in range(1, 8):
-        total = total + recv_a[(j + step) % 8]
-    recv_a[j] = total
+    total = mine[j]
+    for step in range(1, 8):
+        total = total + recv_a[(j + step) % 8].astype(F32)
+    mine[j] = total
     for n in range(8):
-        halves = [recv_a[j, 24 * yt + 2 * n : 24 * yt + 2 * n + 8, :] for yt in range(2)]
+        halves = [mine[j, 24 * yt + 2 * n : 24 * yt + 2 * n + 8, :] for yt in range(2)]
         send_x[n] = jnp.concatenate(halves, axis=0).astype(BF16)
 
     def copy_x(step):
@@ -397,17 +402,17 @@
     for p in range(4):
         d = place_of(p)
         patch = pl.multiple_of(((d % 2) * 2 + r) * 32, 32)
-        mine = dot(sel_q[p], kv[d // 4, :, 0:128])
-        lat_q[32 * p : 32 * p + 32, :] = mine.astype(BF16)
-        both = dot(mine.astype(BF16), gg[...])
-        squares = mine * (both[:, 0:128] + both[:, 128:256] + he2[pl.ds(patch, 32), :])
+        chosen = dot(sel_q[p], kv[d // 4, :, 0:128])
+        lat_q[32 * p : 32 * p + 32, :] = chosen.astype(BF16)
+        both = dot(chosen.astype(BF16), gg[...])
+        squares = chosen * (both[:, 0:128] + both[:, 128:256] + he2[pl.ds(patch, 32), :])
         total = jnp.sum(squares, axis=1, keepdims=True) + ncol[pl.ds(patch, 32), 0:1]
         scales.append(
             lax.rsqrt(jnp.maximum(total, 0.0) * F32(1 / 3072) + F32(1e-06))
             * F32(1 / HS**0.5)
         )
         place = (iota((32, 128), 0) + patch == iota((32, 128), 1)).astype(F32).astype(BF16)
-        tokens.append(jnp.concatenate([mine.astype(BF16), place], axis=1))
+        tokens.append(jnp.concatenate([chosen.astype(BF16), place], axis=1))
     tokens = jnp.concatenate(tokens, axis=0)
     scales = jnp.concatenate(scales, axis=0)
     pltpu.make_async_remote_copy(
@@ -430,89 +435,54 @@
             send_c.at[c, p], recv_c.at[c, p], sc.at[c, p], rc.at[c, p], ring(source_of(p), r), MESH
         )
 
-    near = 2 + r
-
-    def copy_near(c):
-        d = (y + 1 - 2 * (1 - r) + 8) % 8
-        return pltpu.make_async_remote_copy(
-            send_c.at[c, near],
-            recv_c.at[c, near],
-            sc.at[c, near],
-            rc.at[c, near],
-            ring(d, r),
-            MESH,
-        )
-
-    def land_near(c):
-        d = (y - 1 + 2 * (1 - r) + 8) % 8
-        return pltpu.make_async_remote_copy(
-            send_c.at[c, near],
-            recv_c.at[c, near],
-            sc.at[c, near],
-            rc.at[c, near],
-            ring(d, r),
-            MESH,
-        )
-
-    for g in range(2):
-        for p in (2 * g, 2 * g + 1):
-            d = place_of(p)
-            yt = d // 4
-            fi = (d % 4) // 2
-            keys = kv[yt]
-            q = q_all[:, 32 * p : 32 * p + 32, :].reshape(128, 256)
-            scale = jnp.concatenate([key_scale[yt, n] for n in range(4)], axis=1)
-            s = dot_t(q, keys) * scale + bias[yt, fi]
-            top = jnp.max(s, axis=1, keepdims=True)
-            expo = jnp.exp(s - top)
-            norm = jnp.sum(expo, axis=1, keepdims=True)
-            u = dot((expo * scale).astype(BF16), keys) / norm
-            u_all[:, 32 * p : 32 * p + 32, :] = u.reshape(4, 32, 256)
-        if g == 0:
-            pltpu.make_async_remote_copy(
-                fv_all.at[1 - r], fv_all.at[1 - r], sp.at[2], rp.at[2], partner, MESH
-            ).wait_recv()
-            pltpu.make_async_remote_copy(
-                wo.at[1 - r], wo.at[1 - r], sp.at[0], rp.at[0], partner, MESH
-            ).wait_recv()
-        rows = slice(64 * g, 64 * g + 64)
-        for role in range(2):
-            for h in range(2):
-                hi, lo = split2(u_all[2 * role + h, rows, :])
-                cols = slice(HS * h, HS * h + HS)
-                v_hi = fv_all[role, 0, :, cols]
-                v_lo = fv_all[role, 1, :, cols]
-                a = dot(hi, v_hi) + dot(lo, v_hi) + dot(hi, v_lo)
-                a_all[rows, 256 * role + HS * h : 256 * role + HS * h + HS] = a.astype(BF16)
-        for c in range(CHUNKS):
-            cols = slice(width * c, width * c + width)
-            part = dot(a_all[rows, 0:256], wo[0, :, cols]) + dot(
-                a_all[rows, 256:512], wo[1, :, cols]
-            )
-            part = part.reshape(2, 32, width)
-            send_c[c, 2 * g : 2 * g + 2] = part.astype(BF16)
-            if g == 0:
-                copy_c(c, 0).start()
-                copy_c(c, 1).start()
-            else:
-                acc[c] = part
-                copy_near(c).start()
-
-    own_lat = lat_q[pl.ds(pl.multiple_of((3 - r) * 32, 32), 32), :]
+    for p in range(4):
+        d = place_of(p)
+        yt = d // 4
+        fi = (d % 4) // 2
+        keys = kv[yt]
+        q = q_all[:, 32 * p : 32 * p + 32, :].reshape(128, 256)
+        scale = jnp.concatenate([key_scale[yt, n] for n in range(4)], axis=1)
+        s = dot_t(q, keys) * scale + bias[yt, fi]
+        top = jnp.max(s, axis=1, keepdims=True)
+        expo = jnp.exp(s - top)
+        norm = jnp.sum(expo, axis=1, keepdims=True)
+        u = dot((expo * scale).astype(BF16), keys) / norm
+        u_all[:, 32 * p : 32 * p + 32, :] = u.reshape(4, 32, 256)
+    pltpu.make_async_remote_copy(
+        fv_all.at[1 - r], fv_all.at[1 - r], sp.at[2], rp.at[2], partner, MESH
+    ).wait_recv()
+    pltpu.make_async_remote_copy(
+        wo.at[1 - r], wo.at[1 - r], sp.at[0], rp.at[0], partner, MESH
+    ).wait_recv()
+    for role in range(2):
+        for h in range(2):
+            hi, lo = split2(u_all[2 * role + h])
+            cols = slice(HS * h, HS * h + HS)
+            v_hi = fv_all[role, 0, :, cols]
+            v_lo = fv_all[role, 1, :, cols]
+            a = dot(hi, v_hi) + dot(lo, v_hi) + dot(hi, v_lo)
+            a_all[:, 256 * role + HS * h : 256 * role + HS * h + HS] = a.astype(BF16)
+    for c in range(CHUNKS):
+        cols = slice(width * c, width * c + width)
+        part = dot(a_all[:, 0:256], wo[0, :, cols]) + dot(a_all[:, 256:512], wo[1, :, cols])
+        send_c[c] = part[0:96].reshape(3, 32, width).astype(BF16)
+        acc[c] = part[96:128]
+        for p in range(3):
+            copy_c(c, p).start()
+
+    own_lat = lat_q[96:128, :]
     own_patch = pl.multiple_of(((m % 2) * 2 + r) * 32, 32)
     for c in range(CHUNKS):
         cols = slice(width * c, width * c + width)
         embedded = dot(own_lat, e[:, cols]) + pos[pl.ds(own_patch, 32), cols].astype(F32)
-        acc[c, 1 - r] = acc[c, 1 - r] + embedded
+        acc[c] = acc[c] + embedded
     outs = []
     for c in range(CHUNKS):
         cols = slice(width * c, width * c + width)
-        land_c(c, 0).wait_recv()
-        land_c(c, 1).wait_recv()
-        land_near(c).wait_recv()
-        total = acc[c, 1 - r] + recv_c[c, 0].astype(F32)
-        total = total + recv_c[c, 1].astype(F32)
-        total = total + recv_c[c, near].astype(F32)
+        total = acc[c]
+        for p in (1, 2, 0):
+            land_c(c, p).wait_recv()
+            total = total + recv_c[c, p].astype(F32)
         out_ref[:, cols] = total.astype(BF16)
         outs.append(
             pltpu.make_async_copy(out_ref.at[:, cols], out_hbm.at[:, cols], out_sem.at[c])
@@ -534,9 +504,8 @@
     m_copy.wait_send()
     f_copy.wait_send()
     for c in range(CHUNKS):
-        copy_c(c, 0).wait_send()
-        copy_c(c, 1).wait_send()
-        copy_near(c).wait_send()
+        for p in range(3):
+            copy_c(c, p).wait_send()
     for copy in outs:
         copy.wait()
 
@@ -568,7 +537,8 @@
         pltpu.VMEM((2, 256, 3072), BF16),
         pltpu.VMEM((288, 128), F32),
         pltpu.VMEM((8, 48, 128), F32),
-        pltpu.VMEM((8, 48, 128), F32),
+        pltpu.VMEM((8, 48, 128), BF16),
+        pltpu.VMEM((8, 48, 128), BF16),
         pltpu.VMEM((8, 16, 128), BF16),
         pltpu.VMEM((8, 16, 128), BF16),
         pltpu.VMEM((2, 64, 128), BF16),
@@ -589,9 +559,9 @@
         pltpu.VMEM((4, 128, 256), BF16),
         pltpu.VMEM((4, 128, 256), F32),
         pltpu.VMEM((128, 512), BF16),
-        pltpu.VMEM((CHUNKS, 2, 32, width), F32),
-        pltpu.VMEM((CHUNKS, 4, 32, width), BF16),
-        pltpu.VMEM((CHUNKS, 4, 32, width), BF16),
+        pltpu.VMEM((CHUNKS, 32, width), F32),
+        pltpu.VMEM((CHUNKS, 3, 32, width), BF16),
+        pltpu.VMEM((CHUNKS, 3, 32, width), BF16),
         dma((9,)),
         dma((CHUNKS,)),
         dma((8,)),
@@ -604,8 +574,8 @@
         dma((8,)),
         dma((3,)),
         dma((3,)),
-        dma((CHUNKS, 4)),
-        dma((CHUNKS, 4)),
+        dma((CHUNKS, 3)),
+        dma((CHUNKS, 3)),
     ]
     return pl.pallas_call(
         kernel,

time: 62.8 us -> 61.9 us (0.986)
  Pallas kernels: 60.8 us -> 60.1 us
    pallas_call x1, Pallas kernels: 60.8 us -> 60.1 us  [on_device(): pl.pallas_call(kernel, out_shape=jax.ShapeDtypeStruct((32, 3072), BF16),...]
where the time goes in v3:
time: 61.9 us; the launch traced here: 61.7 us
  Pallas kernels  60.1 us (97%)
  local copies, waits for them, and re-layouts  1.62 us (3%)
    pallas_call x1, Pallas kernels, on_device(): pl.pallas_call(kernel, out_shape=jax.ShapeDtypeStruct((32, 3072), BF16),...  60.1 us
    unnamed x1, local copies, waits for them, and re-layouts  1.62 us

profile of v3, /device:TPU:1, one launch (start us, length us, event | category | flops | bytes accessed | tf_op | source)
XLA Modules:
  0.0 61.7 jit_solution(1634473402023987833)
XLA Ops:
  0.0 60.1 %shard_map.91 = bf16[32,3072]{1,0:T(8,128)(2,1)} custom-call(bf16[256,384]{1,0:T(8,128)(2,1)} %bitcast.5, bf16[384,128]{1,0:T(8,128)(2,1)} %gw_hbm.1, s32[1,128]{1,0:T(1,128)} %bitcast.7, s32[256]{0:T(256)} %fb_hbm.1, bf16[128,3072]{1,0:T(8,128)(2,1)} %e_hbm.1, bf16[128,3072]{1,0:T(8,128)(2,1)} %pos_hbm.1, bf16[24,128]{1,0:T(8,128)(2,1)} %bitcast.6, ...), custom_call_target="tpu_custom_call" | custom-call | tf_op jit(solution)/shard_map/pallas_call | solution.py:580
  60.1 1.6 %copy.11 = bf16[32,3072]{1,0:T(8,128)(2,1)} copy(bf16[32,3072]{1,0:T(8,128)(2,1)} %shard_map.91) | data formatting | bytes 393216

commit v4 on v3

--- a/solution.py
+++ b/solution.py
@@ -90,6 +90,8 @@
     acc,
     send_c,
     recv_c,
+    entered,
+    allowed,
     load_sem,
     out_sem,
     sa,
@@ -124,8 +126,8 @@
     def ring(y2, role):
         return ((y2 // 4) * 64 + z * 8 + x, y2 % 4, role)
 
-    def zy_source(idx):
-        return ((idx // 4) * 64 + (2 * (idx % 4) + r) * 8 + x, z // 2, z % 2)
+    def row_z(z2):
+        return (ys * 64 + z2 * 8 + x, m, r)
 
     def zy_dest(i):
         y2 = (y + i) % 8
@@ -136,9 +138,6 @@
 
     def place_of(p):
         return (y + side * offsets[p] + 8) % 8
-
-    def source_of(p):
-        return (y - side * offsets[p] + 8) % 8
 
     partner = (seq, m, 1 - r)
 
@@ -162,19 +161,13 @@
     def greet(device):
         pl.semaphore_signal(barrier, inc=1, device_id=device, device_id_type=MESH)
 
-    for idx in range(8):
-        here = jnp.logical_and(is_self, idx == ys * 4 + z // 2)
-
-        @pl.when(jnp.logical_not(here))
-        def _():
-            greet(zy_source(idx))
-
-    for step in range(1, 8):
+    for step in range(1, 8):
+        greet(row_z((z + step) % 8))
         greet(row_x((x + step) % 8))
     for step in range(1, 8):
-        greet(group((j + step) % 8))
-    for p in range(3):
-        greet(ring(source_of(p), r))
+        greet(ring((y + step) % 8, r))
+    for step in range(8):
+        greet(ring((y + step) % 8, 1 - r))
 
     for copy in (load_po, load_fb, load_gain):
         copy.start()
@@ -190,7 +183,7 @@
         mine[k] = part
         send_a[k] = part.astype(BF16)
 
-    pl.semaphore_wait(barrier, 25 - is_self.astype(jnp.int32))
+    pl.semaphore_wait(barrier, 29)
 
     def copy_a(step):
         k = (j + step) % 8
@@ -206,6 +199,12 @@
 
     for step in range(1, 8):
         copy_a(step).start()
+    for z2 in range(8):
+
+        @pl.when(jnp.logical_and(z2 != z, r == z2 % 2))
+        def _():
+            pl.semaphore_signal(entered.at[z], inc=1, device_id=row_z(z2), device_id_type=MESH)
+
     for copy in (load_e, load_pos, load_w, load_wo):
         copy.start()
     wo_copy = pltpu.make_async_remote_copy(
@@ -282,6 +281,25 @@
 
     for step in range(1, 8):
         land_a(step).wait_recv()
+    @pl.when(r == z % 2)
+    def _():
+        for z2 in range(8):
+
+            @pl.when(z2 != z)
+            def _():
+                pl.semaphore_wait(entered.at[z2], 1)
+
+            for half_y in range(2):
+
+                @pl.when(jnp.logical_not(jnp.logical_and(ys == half_y, j == z2)))
+                def _():
+                    pl.semaphore_signal(
+                        allowed,
+                        inc=1,
+                        device_id=(half_y * 64 + z * 8 + x, z2 // 2, z2 % 2),
+                        device_id_type=MESH,
+                    )
+
     total = mine[j]
     for step in range(1, 8):
         total = total + recv_a[(j + step) % 8].astype(F32)
@@ -329,6 +347,7 @@
         )
 
     local_z = pltpu.make_async_copy(send_z, lat.at[:, half, own_idx], rz.at[own_idx])
+    pl.semaphore_wait(allowed, 8 - (r == z % 2).astype(jnp.int32))
     for i in range(1, 8):
         copy_z(i).start()
 
@@ -426,13 +445,25 @@
     width = 3072 // CHUNKS
 
     def copy_c(c, p):
-        return pltpu.make_async_remote_copy(
-            send_c.at[c, p], recv_c.at[c, p], sc.at[c, p], rc.at[c, p], ring(place_of(p), r), MESH
+        step = -side if p == 1 else side
+        return pltpu.make_async_remote_copy(
+            send_c.at[c, p],
+            recv_c.at[c, p],
+            sc.at[c, p],
+            rc.at[c, p],
+            ring((y + step + 8) % 8, r),
+            MESH,
         )
 
     def land_c(c, p):
-        return pltpu.make_async_remote_copy(
-            send_c.at[c, p], recv_c.at[c, p], sc.at[c, p], rc.at[c, p], ring(source_of(p), r), MESH
+        step = side if p == 1 else -side
+        return pltpu.make_async_remote_copy(
+            send_c.at[c, p],
+            recv_c.at[c, p],
+            sc.at[c, p],
+            rc.at[c, p],
+            ring((y + step + 8) % 8, r),
+            MESH,
         )
 
     for p in range(4):
@@ -465,22 +496,26 @@
     for c in range(CHUNKS):
         cols = slice(width * c, width * c + width)
         part = dot(a_all[:, 0:256], wo[0, :, cols]) + dot(a_all[:, 256:512], wo[1, :, cols])
-        send_c[c] = part[0:96].reshape(3, 32, width).astype(BF16)
-        acc[c] = part[96:128]
-        for p in range(3):
-            copy_c(c, p).start()
+        send_c[c, 0:2] = part[0:64].reshape(2, 32, width).astype(BF16)
+        acc[c] = part[64:128].reshape(2, 32, width)
+        copy_c(c, 0).start()
+        copy_c(c, 1).start()
 
     own_lat = lat_q[96:128, :]
     own_patch = pl.multiple_of(((m % 2) * 2 + r) * 32, 32)
     for c in range(CHUNKS):
         cols = slice(width * c, width * c + width)
         embedded = dot(own_lat, e[:, cols]) + pos[pl.ds(own_patch, 32), cols].astype(F32)
-        acc[c] = acc[c] + embedded
+        acc[c, 1] = acc[c, 1] + embedded
+    for c in range(CHUNKS):
+        land_c(c, 0).wait_recv()
+        send_c[c, 2] = (acc[c, 0] + recv_c[c, 0].astype(F32)).astype(BF16)
+        copy_c(c, 2).start()
     outs = []
     for c in range(CHUNKS):
         cols = slice(width * c, width * c + width)
-        total = acc[c]
-        for p in (1, 2, 0):
+        total = acc[c, 1]
+        for p in (1, 2):
             land_c(c, p).wait_recv()
             total = total + recv_c[c, p].astype(F32)
         out_ref[:, cols] = total.astype(BF16)
@@ -559,9 +594,11 @@
         pltpu.VMEM((4, 128, 256), BF16),
         pltpu.VMEM((4, 128, 256), F32),
         pltpu.VMEM((128, 512), BF16),
-        pltpu.VMEM((CHUNKS, 32, width), F32),
+        pltpu.VMEM((CHUNKS, 2, 32, width), F32),
         pltpu.VMEM((CHUNKS, 3, 32, width), BF16),
         pltpu.VMEM((CHUNKS, 3, 32, width), BF16),
+        pltpu.SemaphoreType.REGULAR((8,)),
+        pltpu.SemaphoreType.REGULAR,
         dma((9,)),
         dma((CHUNKS,)),
         dma((8,)),

time: 61.9 us -> 61.1 us (0.987)
  the two profiles are of different devices: /device:TPU:1 before, /device:TPU:16 now
where the time goes in v4:
time: 61.1 us; the launch traced here: 60.9 us
  Pallas kernels  59.3 us (97%)
  local copies, waits for them, and re-layouts  1.62 us (3%)
    pallas_call x1, Pallas kernels, on_device(): pl.pallas_call(kernel, out_shape=jax.ShapeDtypeStruct((32, 3072), BF16),...  59.3 us
    unnamed x1, local copies, waits for them, and re-layouts  1.62 us

profile of v4, /device:TPU:16, one launch (start us, length us, event | category | flops | bytes accessed | tf_op | source)
XLA Modules:
  0.0 60.9 jit_solution(10031667385002483530)
XLA Ops:
  0.0 59.3 %shard_map.91 = bf16[32,3072]{1,0:T(8,128)(2,1)} custom-call(bf16[256,384]{1,0:T(8,128)(2,1)} %bitcast.5, bf16[384,128]{1,0:T(8,128)(2,1)} %gw_hbm.1, s32[1,128]{1,0:T(1,128)} %bitcast.7, s32[256]{0:T(256)} %fb_hbm.1, bf16[128,3072]{1,0:T(8,128)(2,1)} %e_hbm.1, bf16[128,3072]{1,0:T(8,128)(2,1)} %pos_hbm.1, bf16[24,128]{1,0:T(8,128)(2,1)} %bitcast.6, ...), custom_call_target="tpu_custom_call" | custom-call | tf_op jit(solution)/shard_map/pallas_call | solution.py:617
  59.3 1.6 %copy.11 = bf16[32,3072]{1,0:T(8,128)(2,1)} copy(bf16[32,3072]{1,0:T(8,128)(2,1)} %shard_map.91) | data formatting | bytes 393216

commit v5 on v4

--- a/solution.py
+++ b/solution.py
@@ -248,6 +248,55 @@
         )
         sel_q[p] = hit.astype(F32).astype(BF16)
 
+    def weight_product(c):
+        both = dot(fhl[...], w[c])
+        return both[0:256] + both[256:512]
+
+    for step in range(1, 8):
+        land_a(step).wait_recv()
+    @pl.when(r == z % 2)
+    def _():
+        for z2 in range(8):
+
+            @pl.when(z2 != z)
+            def _():
+                pl.semaphore_wait(entered.at[z2], 1)
+
+            for half_y in range(2):
+
+                @pl.when(jnp.logical_not(jnp.logical_and(ys == half_y, j == z2)))
+                def _():
+                    pl.semaphore_signal(
+                        allowed,
+                        inc=1,
+                        device_id=(half_y * 64 + z * 8 + x, z2 // 2, z2 % 2),
+                        device_id_type=MESH,
+                    )
+
+    total = mine[j]
+    for step in range(1, 8):
+        total = total + recv_a[(j + step) % 8].astype(F32)
+    mine[j] = total
+    for n in range(8):
+        halves = [mine[j, 24 * yt + 2 * n : 24 * yt + 2 * n + 8, :] for yt in range(2)]
+        send_x[n] = jnp.concatenate(halves, axis=0).astype(BF16)
+
+    def copy_x(step):
+        x2 = (x + step) % 8
+        return pltpu.make_async_remote_copy(
+            send_x.at[x2], recv_x.at[x], sx.at[step], rx.at[x], row_x(x2), MESH
+        )
+
+    def land_x(step):
+        x2 = (x + step) % 8
+        return pltpu.make_async_remote_copy(
+            send_x.at[x2], recv_x.at[x2], sx.at[step], rx.at[x2], row_x(x2), MESH
+        )
+
+    for step in range(1, 8):
+        copy_x(step).start()
+    recv_x[x] = send_x[x]
+
     load_e.wait()
     load_pos.wait()
     load_gain.wait()
@@ -275,58 +324,6 @@
     load_w.wait()
     load_wo.wait()
 
-    def weight_product(c):
-        both = dot(fhl[...], w[c])
-        return both[0:256] + both[256:512]
-
-    for step in range(1, 8):
-        land_a(step).wait_recv()
-    @pl.when(r == z % 2)
-    def _():
-        for z2 in range(8):
-
-            @pl.when(z2 != z)
-            def _():
-                pl.semaphore_wait(entered.at[z2], 1)
-
-            for half_y in range(2):
-
-                @pl.when(jnp.logical_not(jnp.logical_and(ys == half_y, j == z2)))
-                def _():
-                    pl.semaphore_signal(
-                        allowed,
-                        inc=1,
-                        device_id=(half_y * 64 + z * 8 + x, z2 // 2, z2 % 2),
-                        device_id_type=MESH,
-                    )
-
-    total = mine[j]
-    for step in range(1, 8):
-        total = total + recv_a[(j + step) % 8].astype(F32)
-    mine[j] = total
-    for n in range(8):
-        halves = [mine[j, 24 * yt + 2 * n : 24 * yt + 2 * n + 8, :] for yt in range(2)]
-        send_x[n] = jnp.concatenate(halves, axis=0).astype(BF16)
-
-    def copy_x(step):
-        x2 = (x + step) % 8
-        return pltpu.make_async_remote_copy(
-            send_x.at[x2], recv_x.at[x], sx.at[step], rx.at[x], row_x(x2), MESH
-        )
-
-    def land_x(step):
-        x2 = (x + step) % 8
-        return pltpu.make_async_remote_copy(
-            send_x.at[x2], recv_x.at[x2], sx.at[step], rx.at[x2], row_x(x2), MESH
-        )
-
-    for step in range(1, 8):
-        copy_x(step).start()
-    recv_x[x] = send_x[x]
-
-    fq = weight_product(0)
-    fk = weight_product(1)
-
     for step in range(1, 8):
         land_x(step).wait_recv()
     for a in range(4):
@@ -359,6 +356,8 @@
     def _():
         local_z.start()
 
+    fq = weight_product(0)
+    fk = weight_product(1)
     for h in range(2):
         cols = slice(HS * h, HS * h + HS)
         bil = dot_t(fq[:, cols], fk[:, cols], lax.Precision.HIGHEST)
@@ -389,7 +388,7 @@
             block, block, sf.at[idx], rf.at[idx], partner, MESH
         )
 
-    ones = jnp.ones((8, 128), F32)
+    ones = jnp.ones((16, 128), F32).astype(BF16)
 
     def take_batch(parity, n):
         batch = parity * 2 + n
@@ -399,8 +398,8 @@
             kv[yt, pl.ds(first, 256), 0:128] = rows
             both = dot(rows, gg[...])
             cross = both[:, 0:128] + both[:, 128:256] + hr2[pl.ds(first, 256), :]
-            total = dot_t(ones, rows.astype(F32) * cross, lax.Precision.HIGHEST)[0:1]
-            total = total + nlane[batch]
+            hi, lo = split2(rows.astype(F32) * cross)
+            total = dot_t(ones, hi)[0:1] + dot_t(ones, lo)[0:1] + nlane[batch]
             key_scale[yt, batch] = lax.rsqrt(
                 jnp.maximum(total, 0.0) * F32(1 / 3072) + F32(1e-06)
             )
@@ -411,7 +410,6 @@
             pltpu.make_async_copy(block, block, rz.at[idx]).wait()
             forward(idx).start()
         take_batch(r, n)
-    for n in range(2):
         for idx in range(4 * n, 4 * n + 4):
             forwarded(idx).wait_recv()
         take_batch(1 - r, n)
@@ -466,7 +464,7 @@
             MESH,
         )
 
-    for p in range(4):
+    def attend(p):
         d = place_of(p)
         yt = d // 4
         fi = (d % 4) // 2
@@ -479,26 +477,39 @@
         norm = jnp.sum(expo, axis=1, keepdims=True)
         u = dot((expo * scale).astype(BF16), keys) / norm
         u_all[:, 32 * p : 32 * p + 32, :] = u.reshape(4, 32, 256)
+
+    def heads_out(rows):
+        for role in range(2):
+            for h in range(2):
+                hi, lo = split2(u_all[2 * role + h, rows, :])
+                cols = slice(HS * h, HS * h + HS)
+                v_hi = fv_all[role, 0, :, cols]
+                v_lo = fv_all[role, 1, :, cols]
+                a = dot(hi, v_hi) + dot(lo, v_hi) + dot(hi, v_lo)
+                a_all[rows, 256 * role + HS * h : 256 * role + HS * h + HS] = a.astype(BF16)
+
+    def projected(rows, c):
+        cols = slice(width * c, width * c + width)
+        return dot(a_all[rows, 0:256], wo[0, :, cols]) + dot(a_all[rows, 256:512], wo[1, :, cols])
+
     pltpu.make_async_remote_copy(
         fv_all.at[1 - r], fv_all.at[1 - r], sp.at[2], rp.at[2], partner, MESH
     ).wait_recv()
     pltpu.make_async_remote_copy(
         wo.at[1 - r], wo.at[1 - r], sp.at[0], rp.at[0], partner, MESH
     ).wait_recv()
-    for role in range(2):
-        for h in range(2):
-            hi, lo = split2(u_all[2 * role + h])
-            cols = slice(HS * h, HS * h + HS)
-            v_hi = fv_all[role, 0, :, cols]
-            v_lo = fv_all[role, 1, :, cols]
-            a = dot(hi, v_hi) + dot(lo, v_hi) + dot(hi, v_lo)
-            a_all[:, 256 * role + HS * h : 256 * role + HS * h + HS] = a.astype(BF16)
+    attend(0)
+    heads_out(slice(0, 32))
     for c in range(CHUNKS):
-        cols = slice(width * c, width * c + width)
-        part = dot(a_all[:, 0:256], wo[0, :, cols]) + dot(a_all[:, 256:512], wo[1, :, cols])
-        send_c[c, 0:2] = part[0:64].reshape(2, 32, width).astype(BF16)
-        acc[c] = part[64:128].reshape(2, 32, width)
+        send_c[c, 0] = projected(slice(0, 32), c).astype(BF16)
         copy_c(c, 0).start()
+    for p in range(1, 4):
+        attend(p)
+    heads_out(slice(32, 128))
+    for c in range(CHUNKS):
+        part = projected(slice(32, 128), c)
+        send_c[c, 1] = part[0:32].astype(BF16)
+        acc[c] = part[32:96].reshape(2, 32, width)
         copy_c(c, 1).start()
 
     own_lat = lat_q[96:128, :]

time: 61.1 us -> 59.9 us (0.980)
  the two profiles are of different devices: /device:TPU:16 before, /device:TPU:1 now
where the time goes in v5:
time: 59.9 us; the launch traced here: 59.7 us
  Pallas kernels  58.1 us (97%)
  local copies, waits for them, and re-layouts  1.62 us (3%)
    pallas_call x1, Pallas kernels, on_device(): pl.pallas_call(kernel, out_shape=jax.ShapeDtypeStruct((32, 3072), BF16),...  58.1 us
    unnamed x1, local copies, waits for them, and re-layouts  1.62 us

profile of v5, /device:TPU:1, one launch (start us, length us, event | category | flops | bytes accessed | tf_op | source)
XLA Modules:
  0.0 59.7 jit_solution(9781327411025374129)
XLA Ops:
  0.0 58.1 %shard_map.91 = bf16[32,3072]{1,0:T(8,128)(2,1)} custom-call(bf16[256,384]{1,0:T(8,128)(2,1)} %bitcast.5, bf16[384,128]{1,0:T(8,128)(2,1)} %gw_hbm.1, s32[1,128]{1,0:T(1,128)} %bitcast.7, s32[256]{0:T(256)} %fb_hbm.1, bf16[128,3072]{1,0:T(8,128)(2,1)} %e_hbm.1, bf16[128,3072]{1,0:T(8,128)(2,1)} %pos_hbm.1, bf16[24,128]{1,0:T(8,128)(2,1)} %bitcast.6, ...), custom_call_target="tpu_custom_call" | custom-call | tf_op jit(solution)/shard_map/pallas_call | solution.py:628
  58.1 1.6 %copy.11 = bf16[32,3072]{1,0:T(8,128)(2,1)} copy(bf16[32,3072]{1,0:T(8,128)(2,1)} %shard_map.91) | data formatting | bytes 393216

commit v6 on v5

--- a/solution.py
+++ b/solution.py
@@ -11,7 +11,8 @@
 F32 = jnp.float32
 BF16 = jnp.bfloat16
 HS = 128
-CHUNKS = 4
+CHUNKS = 6
+FAR_FIRST = (4, 3, 5, 2, 6, 1, 7)
 NEG = -1e30
 
 
@@ -161,13 +162,12 @@
     def greet(device):
         pl.semaphore_signal(barrier, inc=1, device_id=device, device_id_type=MESH)
 
-    for step in range(1, 8):
+    for step in FAR_FIRST:
         greet(row_z((z + step) % 8))
         greet(row_x((x + step) % 8))
-    for step in range(1, 8):
         greet(ring((y + step) % 8, r))
-    for step in range(8):
         greet(ring((y + step) % 8, 1 - r))
+    greet(partner)
 
     for copy in (load_po, load_fb, load_gain):
         copy.start()
@@ -293,7 +293,7 @@
             send_x.at[x2], recv_x.at[x2], sx.at[step], rx.at[x2], row_x(x2), MESH
         )
 
-    for step in range(1, 8):
+    for step in FAR_FIRST:
         copy_x(step).start()
     recv_x[x] = send_x[x]
 
@@ -345,7 +345,7 @@
 
     local_z = pltpu.make_async_copy(send_z, lat.at[:, half, own_idx], rz.at[own_idx])
     pl.semaphore_wait(allowed, 8 - (r == z % 2).astype(jnp.int32))
-    for i in range(1, 8):
+    for i in FAR_FIRST:
         copy_z(i).start()
 
     @pl.when(jnp.logical_not(is_self))

time: 59.9 us -> 59.8 us (level)
  no operation moved by 1% of the time
where the time goes in v6:
time: 59.8 us; the launch traced here: 59.6 us
  Pallas kernels  58 us (97%)
  local copies, waits for them, and re-layouts  1.62 us (3%)
    pallas_call x1, Pallas kernels, on_device(): pl.pallas_call(kernel, out_shape=jax.ShapeDtypeStruct((32, 3072), BF16),...  58 us
    unnamed x1, local copies, waits for them, and re-layouts  1.62 us

profile of v6, /device:TPU:1, one launch (start us, length us, event | category | flops | bytes accessed | tf_op | source)
XLA Modules:
  0.0 59.6 jit_solution(15438363460947740531)
XLA Ops:
  0.0 58.0 %shard_map.91 = bf16[32,3072]{1,0:T(8,128)(2,1)} custom-call(bf16[256,384]{1,0:T(8,128)(2,1)} %bitcast.5, bf16[384,128]{1,0:T(8,128)(2,1)} %gw_hbm.1, s32[1,128]{1,0:T(1,128)} %bitcast.7, s32[256]{0:T(256)} %fb_hbm.1, bf16[128,3072]{1,0:T(8,128)(2,1)} %e_hbm.1, bf16[128,3072]{1,0:T(8,128)(2,1)} %pos_hbm.1, bf16[24,128]{1,0:T(8,128)(2,1)} %bitcast.6, ...), custom_call_target="tpu_custom_call" | custom-call | tf_op jit(solution)/shard_map/pallas_call | solution.py:628
  58.0 1.6 %copy.11 = bf16[32,3072]{1,0:T(8,128)(2,1)} copy(bf16[32,3072]{1,0:T(8,128)(2,1)} %shard_map.91) | data formatting | bytes 393216
